TPU v7x, 256 devices: a whole 4x4x8 slice. The times are simulated.
256 devices in a mesh: row: 16 (over z, y_hi), col: 16 (over y_lo, x, core).
Axes of the slice: x: 4, y: 4 (y_hi: 2, y_lo: 2; y = y_hi * 2 + y_lo), z: 8, core: 2. Of those that a mesh axis runs over, the one named last changes fastest.
Arguments:
- object_field: float32 [2, 4096, 4096], P(None, 'row', 'col'), may hold values from -5 to 5
- probe: float32 [2, 256, 256], replicated, may hold values from -6 to 6
- amplitudes: float32 [16, 16, 4, 256, 256], P('row', 'col'), may hold values from 0 to 11, as said below
- positions: int32 [16, 16, 4, 2], P('row', 'col'), may hold values from 0 to 64
Outputs:
- object_next: float32 [2, 4096, 4096], P(None, 'row', 'col')
- probe_next: float32 [2, 256, 256], replicated
Inputs may be any that keep to these rules, and one draw needn't show every extreme that they name: Positive amplitudes.
All inputs are finite; a program needn't handle non-finite values.
Results may differ from a plain program's by a relative error of at most 0.0003.
Values sent between devices are 32-bit elements; how exact they have to be, the bound alone decides.
A program may use at most 64 MiB of HBM per device.

v0:
```python
import math

import jax
import jax.numpy as jnp
from jax import lax
from jax.sharding import PartitionSpec as P

W = 256
MARGIN = 32


smoothing = 0.1
regular = 1.0
epsilon = 1e-06


def padded(block, sides, width):
    for axis, dim in sides:
        count = lax.axis_size(axis)
        forward = [(i, i + 1) for i in range(count - 1)]
        backward = [(target, source) for source, target in forward]
        low = lax.ppermute(
            lax.slice_in_dim(block, block.shape[dim] - width, None, axis=dim), axis, forward
        )
        high = lax.ppermute(lax.slice_in_dim(block, 0, width, axis=dim), axis, backward)
        block = jnp.concatenate([low, block, high], axis=dim)
    return block


def shifted(block, axis, distance):
    devices = range(lax.axis_size(axis))
    route = [(i - distance, i) for i in devices if i - distance in devices]
    return lax.ppermute(block, axis, route)


def tables(length):
    indices = jnp.arange(length, dtype=jnp.int32)
    phases = (indices[:, None] * indices[None, :] % length).astype(jnp.float32) * (
        2.0 * math.pi / length
    )
    scaling = 1.0 / math.sqrt(length)
    cosine = jnp.cos(phases) * scaling
    sines = jnp.sin(phases) * scaling
    forward = jnp.concatenate(
        [jnp.concatenate([cosine, sines], 1), jnp.concatenate([-sines, cosine], 1)], 0
    )
    inverse = jnp.concatenate(
        [jnp.concatenate([cosine, -sines], 1), jnp.concatenate([sines, cosine], 1)], 0
    )
    return (forward, inverse)


def transform(wavefield, left_matrix, right_matrix):
    length = wavefield.shape[1]
    stacked = wavefield.reshape(2 * length, length)
    mixed = jnp.dot(left_matrix, stacked, precision=lax.Precision.HIGHEST)
    paired = jnp.concatenate([mixed[:length], mixed[length:]], axis=1)
    result = jnp.dot(paired, right_matrix, precision=lax.Precision.HIGHEST)
    return jnp.stack([result[:, :length], result[:, length:]])


def frame_terms(probe, window, amplitude, forward, inverse):
    exit_real = probe[0] * window[0] - probe[1] * window[1]
    exit_imag = probe[0] * window[1] + probe[1] * window[0]
    wave = jnp.stack([exit_real, exit_imag])
    far_field = transform(wave, forward, inverse)
    factor = amplitude / jnp.sqrt(
        far_field[0] * far_field[0] + far_field[1] * far_field[1] + smoothing
    )
    near_field = transform(far_field * factor[None], inverse, forward)
    difference = near_field - wave
    object_real = probe[0] * difference[0] + probe[1] * difference[1]
    object_imag = probe[0] * difference[1] - probe[1] * difference[0]
    probe_real = window[0] * difference[0] + window[1] * difference[1]
    probe_imag = window[0] * difference[1] - window[1] * difference[0]
    window_power = window[0] * window[0] + window[1] * window[1]
    return (
        jnp.stack([object_real, object_imag]),
        jnp.stack([probe_real, probe_imag, window_power]),
    )


def add_edges(middle, leading, trailing, along, tile_side, margin):
    head_pad = [(0, 0), (0, 0), (0, 0)]
    tail_pad = [(0, 0), (0, 0), (0, 0)]
    head_pad[along] = (0, tile_side - margin)
    tail_pad[along] = (tile_side - margin, 0)
    return middle + jnp.pad(leading, head_pad) + jnp.pad(trailing, tail_pad)


def per_device(object_field, probe, amplitudes, positions):
    forward, inverse = tables(W)
    tile_side = object_field.shape[1]
    margin = MARGIN
    window_side = tile_side + 2 * margin
    extended = padded(object_field, (("row", 1), ("col", 2)), MARGIN)
    power_map = probe[0] * probe[0] + probe[1] * probe[1]
    measured = amplitudes[0, 0]
    offsets = positions[0, 0]
    frame_total = measured.shape[0]
    anchor = jnp.zeros((), jnp.int32)

    def visit(frame_index, carried):
        canvas, probe_acc = carried
        amplitude = measured[frame_index]
        offset = offsets[frame_index]
        window = lax.dynamic_slice(extended, (anchor, offset[0], offset[1]), (2, W, W))
        object_term, probe_term = frame_terms(probe, window, amplitude, forward, inverse)
        update = jnp.concatenate([object_term, power_map[None]], 0)
        current = lax.dynamic_slice(canvas, (anchor, offset[0], offset[1]), (3, W, W))
        canvas = lax.dynamic_update_slice(canvas, current + update, (anchor, offset[0], offset[1]))
        return (canvas, probe_acc + probe_term)

    canvas_start = jnp.zeros((3, window_side, window_side), jnp.float32)
    probe_start = jnp.zeros((3, W, W), jnp.float32)
    canvas, probe_acc = lax.fori_loop(0, frame_total, visit, (canvas_start, probe_start))
    from_above = shifted(canvas[:, window_side - margin :, :], "row", 1)
    from_below = shifted(canvas[:, :margin, :], "row", -1)
    row_folded = add_edges(
        canvas[:, margin : margin + tile_side, :], from_above, from_below, 1, tile_side, margin
    )
    from_before = shifted(row_folded[:, :, window_side - margin :], "col", 1)
    from_after = shifted(row_folded[:, :, :margin], "col", -1)
    folded = add_edges(
        row_folded[:, :, margin : margin + tile_side], from_before, from_after, 2, tile_side, margin
    )
    object_next = object_field + folded[0:2] / (folded[2] + regular)
    local_target = jnp.sum(measured * measured)
    devices = lax.axis_size("row") * lax.axis_size("col")
    frame_count = frame_total * devices
    totals, target_sum = lax.psum((probe_acc, local_target), ("row", "col"))
    stepped = probe + totals[0:2] / (totals[2] + regular)
    probe_power = jnp.sum(stepped * stepped)
    target = target_sum / frame_count
    probe_next = stepped * jnp.sqrt(target / (probe_power + epsilon))
    return (object_next, probe_next)


def solution(mesh):
    return jax.shard_map(
        per_device,
        mesh=mesh,
        in_specs=(
            P(None, "row", "col"),
            P(),
            P("row", "col", None, None, None),
            P("row", "col", None, None),
        ),
        out_specs=(P(None, "row", "col"), P()),
        check_vma=False,
    )
```

profile of v0, /device:TPU:1, one launch (start us, length us, event | category | flops | bytes accessed | tf_op | source)
XLA Modules:
  0.0 515.6 jit_solution(1246306254406606753)
XLA Ops:
  8.2 5.6 %collective-permute-start = (f32[2,32,256]{2,1,0:T(8,128)S(1)}, f32[2,32,256]{2,1,0:T(8,128)S(1)}, u32[]{:S(2)}, u32[]{:S(2)}) collective-permute-start(f32[2,32,256]{2,1,0:T(8,128)S(1)} %get-tuple-element.258), channel_id=1, source_target_pairs={{0,16},{16,32},{32,48},{48,64},{64,80},{80,96},{96,112},{112,128},... | collective-permute-start | bytes 196616 | tf_op jit(solution)/shard_map/ppermute | solution.py:22
  13.8 1.3 collective-permute-start.1
  16.2 1.8 add_bitcast_fusion
  19.0 1.3 collective-permute-done.1
  21.2 5.1 collective-permute-start.2
  26.4 1.9 collective-permute-start.3
  28.5 2.1 collective-permute-done.2
  30.7 4.4 collective-permute-done.3
  35.1 2.4 pad_maximum_fusion.5
  37.5 1.2 broadcast_in_dim.20
  38.7 108.4 %while.16 = (s32[]{:T(128)}, f32[3,320,320]{2,1,0:T(8,128)}, f32[3,256,256]{2,1,0:T(8,128)}, s32[4,2]{0,1:T(2,128)S(1)}, f32[2,256,256]{2,1,0:T(8,128)S(1)}, /*i...) while((s32[]{:T(128)}, f32[3,320,320]{2,1,0:T(8,128)}, ...), condition=%wide.region_1.2_spmd.clone, body=%wide.region_0.1_spmd.clone.sunk | while | flops 3225354240 | bytes 31064388 | solution.py:116
  43.2 1.3 multiply_subtract_fusion.4
  44.6 1.9 convolution_bitcast_fusion.4
  48.7 1.9 convolution_bitcast_fusion.5
  51.8 1.1 copy-done.1
  52.9 1.3 multiply_add_fusion.5
  54.1 2.9 maximum_add_fusion.3
  57.1 8.4 %dynamic_update_slice.9 = f32[3,320,320]{2,1,0:T(8,128)} dynamic-update-slice(f32[3,320,320]{2,1,0:T(8,128)} %get-tuple-element.377, f32[3,256,256]{2,1,0:T(8,128)S(1)} %get-tuple-element.360, s32[]{:T(128)} %constant.57.clone.1..sunk, s32[]{:T(128)S(6)} %select_n.61, s32[]{:T(128)S(6)} %select_n.62) | dynamic-update-slice | bytes 1572868 | tf_op jit(solution)/shard_map/while/body/eval_jaxpr/dynamic_update_slice | solution.py:111
  70.0 1.3 multiply_subtract_fusion.4
  71.4 1.9 convolution_bitcast_fusion.4
  75.5 1.9 convolution_bitcast_fusion.5
  78.6 1.1 copy-done.1
  79.7 1.3 multiply_add_fusion.5
  80.9 3.2 maximum_add_fusion.3
  84.1 8.7 %dynamic_update_slice.9 = f32[3,320,320]{2,1,0:T(8,128)} dynamic-update-slice(f32[3,320,320]{2,1,0:T(8,128)} %get-tuple-element.377, f32[3,256,256]{2,1,0:T(8,128)S(1)} %get-tuple-element.360, s32[]{:T(128)} %constant.57.clone.1..sunk, s32[]{:T(128)S(6)} %select_n.61, s32[]{:T(128)S(6)} %select_n.62) | dynamic-update-slice | bytes 1572868 | tf_op jit(solution)/shard_map/while/body/eval_jaxpr/dynamic_update_slice | solution.py:111
  97.3 1.3 multiply_subtract_fusion.4
  98.7 1.9 convolution_bitcast_fusion.4
  102.8 1.9 convolution_bitcast_fusion.5
  106.9 1.3 multiply_add_fusion.5
  108.2 3.2 maximum_add_fusion.3
  111.4 8.6 %dynamic_update_slice.9 = f32[3,320,320]{2,1,0:T(8,128)} dynamic-update-slice(f32[3,320,320]{2,1,0:T(8,128)} %get-tuple-element.377, f32[3,256,256]{2,1,0:T(8,128)S(1)} %get-tuple-element.360, s32[]{:T(128)} %constant.57.clone.1..sunk, s32[]{:T(128)S(6)} %select_n.61, s32[]{:T(128)S(6)} %select_n.62) | dynamic-update-slice | bytes 1572868 | tf_op jit(solution)/shard_map/while/body/eval_jaxpr/dynamic_update_slice | solution.py:111
  124.5 1.3 multiply_subtract_fusion.4
  125.9 1.9 convolution_bitcast_fusion.4
  130.0 1.9 convolution_bitcast_fusion.5
  133.1 1.1 copy-done.1
  134.2 1.3 multiply_add_fusion.5
  135.5 3.2 maximum_add_fusion.3
  138.7 8.5 %dynamic_update_slice.9 = f32[3,320,320]{2,1,0:T(8,128)} dynamic-update-slice(f32[3,320,320]{2,1,0:T(8,128)} %get-tuple-element.377, f32[3,256,256]{2,1,0:T(8,128)S(1)} %get-tuple-element.360, s32[]{:T(128)} %constant.57.clone.1..sunk, s32[]{:T(128)S(6)} %select_n.61, s32[]{:T(128)S(6)} %select_n.62) | dynamic-update-slice | bytes 1572868 | tf_op jit(solution)/shard_map/while/body/eval_jaxpr/dynamic_update_slice | solution.py:111
  148.2 4.5 collective-permute-start.4
  152.7 1.4 collective-permute-start.5
  154.1 2.2 collective-permute-done.4
  156.3 3.9 collective-permute-done.5
  160.2 1.4 pad_add_fusion
  161.7 4.2 collective-permute-start.6
  165.9 1.9 collective-permute-start.7
  168.7 82.9 %psum.15 = f32[]{:T(128)} all-reduce(f32[]{:T(128)} %multiply_reduce_fusion), channel_id=1, replica_groups=mesh['row'=16,'col'=16] {'row','col'}, use_global_device_ids=true, to_apply=%region_4.5 | all-reduce | flops 1 | bytes 8 | tf_op jit(solution)/shard_map/psum | solution.py:131
  254.2 250.1 %all-reduce.6.cloned.1.call-done = f32[3,256,256]{2,1,0:T(8,128)} async-done(((f32[3,256,256]{2,1,0:T(8,128)}), f32[3,256,256]{2,1,0:T(8,128)}) %all-reduce.6.cloned.1.call-update) | async-done | bytes 786448 | tf_op jit(solution)/shard_map/psum | solution.py:131
  505.3 1.8 multiply_reduce_fusion.1
  (83 shorter events, 27.2 us)
Async XLA Ops:
  7.2 11.8 %copy-start.3 = (f32[2,256,256]{2,1,0:T(8,128)S(1)}, f32[2,256,256]{2,1,0:T(8,128)}, u32[]{:S(2)}) copy-start(f32[2,256,256]{2,1,0:T(8,128)} %param.6) | copy-start | bytes 1572868
  7.2 497.1 %all-reduce.6.cloned.1.call-start = ((), (), s32[]{:S(2)}) async-start(), calls=%async_computation | async-start | bytes 1572864 | tf_op jit(solution)/shard_map/psum | solution.py:131
  8.2 10.8 %collective-permute-start = (f32[2,32,256]{2,1,0:T(8,128)S(1)}, f32[2,32,256]{2,1,0:T(8,128)S(1)}, u32[]{:S(2)}, u32[]{:S(2)}) collective-permute-start(f32[2,32,256]{2,1,0:T(8,128)S(1)} %get-tuple-element.258), channel_id=1, source_target_pairs={{0,16},{16,32},{32,48},{48,64},{64,80},{80,96},{96,112},{112,128},... | collective-permute-start | bytes 196616 | tf_op jit(solution)/shard_map/ppermute | solution.py:22
  13.8 6.5 %collective-permute-start.1 = (f32[2,32,256]{2,1,0:T(8,128)S(1)}, f32[2,32,256]{2,1,0:T(8,128)S(1)}, u32[]{:S(2)}, u32[]{:S(2)}) collective-permute-start(f32[2,32,256]{2,1,0:T(8,128)S(1)} %get-tuple-element.257), channel_id=1, source_target_pairs={{16,0},{32,16},{48,32},{64,48},{80,64},{96,80},{112,96},{128,112},... | collective-permute-start | bytes 196616 | tf_op jit(solution)/shard_map/ppermute | solution.py:25
  21.2 9.4 %collective-permute-start.2 = (f32[2,320,32]{2,1,0:T(8,128)}, f32[2,320,32]{2,1,0:T(8,128)}, u32[]{:S(2)}, u32[]{:S(2)}) collective-permute-start(f32[2,320,32]{2,1,0:T(8,128)} %get-tuple-element.255), channel_id=1, source_target_pairs={{0,1},{1,2},{2,3},{3,4},{4,5},{5,6},{6,7},{7,8},{8,9},{9,10},{10,1... | collective-permute-start | bytes 245768 | tf_op jit(solution)/shard_map/ppermute | solution.py:22
  26.4 8.7 %collective-permute-start.3 = (f32[2,320,32]{2,1,0:T(8,128)}, f32[2,320,32]{2,1,0:T(8,128)}, u32[]{:S(2)}, u32[]{:S(2)}) collective-permute-start(f32[2,320,32]{2,1,0:T(8,128)} %get-tuple-element.256), channel_id=1, source_target_pairs={{1,0},{2,1},{3,2},{4,3},{5,4},{6,5},{7,6},{8,7},{9,8},{10,9},{11,1... | collective-permute-start | bytes 245768 | tf_op jit(solution)/shard_map/ppermute | solution.py:25
  28.5 10.2 %copy-start = (f32[2,256,256]{2,1,0:T(8,128)S(1)}, f32[2,256,256]{2,1,0:T(8,128)}, u32[]{:S(2)}) copy-start(f32[2,256,256]{2,1,0:T(8,128)} %param.7) | copy-start | bytes 1572868
  28.5 10.2 %copy-start.6 = (s32[1,1,4,2]{2,3,1,0:T(2,128)S(1)}, s32[1,1,4,2]{2,3,1,0:T(2,128)}, u32[]{:S(2)}) copy-start(s32[1,1,4,2]{2,3,1,0:T(2,128)} %param.9) | copy-start | bytes 100
  51.7 1.2 copy-start.1
  78.5 1.2 copy-start.1
  105.7 1.2 copy-start.1
  133.0 1.2 copy-start.1
  148.2 8.1 %collective-permute-start.4 = (f32[3,32,320]{2,1,0:T(8,128)S(1)}, f32[3,32,320]{2,1,0:T(8,128)S(1)}, u32[]{:S(2)}, u32[]{:S(2)}) collective-permute-start(f32[3,32,320]{2,1,0:T(8,128)S(1)} %get-tuple-element.249), channel_id=1, source_target_pairs={{0,16},{16,32},{32,48},{48,64},{64,80},{80,96},{96,112},{112,128},... | collective-permute-start | bytes 368648 | tf_op jit(solution)/shard_map/ppermute | solution.py:33
  152.6 15.2 %copy-start.2 = (f32[4,256,256]{2,1,0:T(8,128)S(1)}, f32[4,256,256]{2,1,0:T(8,128)}, u32[]{:S(2)}) copy-start(f32[4,256,256]{2,1,0:T(8,128)} %get-tuple-element.408) | copy-start | bytes 3145732
  152.7 7.5 %collective-permute-start.5 = (f32[3,32,320]{2,1,0:T(8,128)S(1)}, f32[3,32,320]{2,1,0:T(8,128)S(1)}, u32[]{:S(2)}, u32[]{:S(2)}) collective-permute-start(f32[3,32,320]{2,1,0:T(8,128)S(1)} %get-tuple-element.250), channel_id=1, source_target_pairs={{16,0},{32,16},{48,32},{64,48},{80,64},{96,80},{112,96},{128,112},... | collective-permute-start | bytes 368648 | tf_op jit(solution)/shard_map/ppermute | solution.py:33
  161.7 90.6 %collective-permute-start.6 = (f32[3,256,32]{2,1,0:T(8,128)S(1)}, f32[3,256,32]{2,1,0:T(8,128)S(1)}, u32[]{:S(2)}, u32[]{:S(2)}) collective-permute-start(f32[3,256,32]{2,1,0:T(8,128)S(1)} %get-tuple-element.251), channel_id=1, source_target_pairs={{0,1},{1,2},{2,3},{3,4},{4,5},{5,6},{6,7},{7,8},{8,9},{9,10},{10,1... | collective-permute-start | bytes 294920 | tf_op jit(solution)/shard_map/ppermute | solution.py:33
  165.9 86.4 %collective-permute-start.7 = (f32[3,256,32]{2,1,0:T(8,128)S(1)}, f32[3,256,32]{2,1,0:T(8,128)S(1)}, u32[]{:S(2)}, u32[]{:S(2)}) collective-permute-start(f32[3,256,32]{2,1,0:T(8,128)S(1)} %get-tuple-element.252), channel_id=1, source_target_pairs={{1,0},{2,1},{3,2},{4,3},{5,4},{6,5},{7,6},{8,7},{9,8},{10,9},{11,1... | collective-permute-start | bytes 294920 | tf_op jit(solution)/shard_map/ppermute | solution.py:33
  252.3 1.0 copy-start.4
  504.3 3.6 copy-start.5
Sparse Core Ops, SparseCore 0:
  252.4 251.8 all-reduce.5
where the time goes:
time: 519 us; the launch traced here: 516 us
  waiting for transfers between devices  264 us (51%)
  blocking collectives  82.9 us (16%)
  local copies, waits for them, and re-layouts  46.3 us (9%)
  other arithmetic  41.5 us (8%)
  starting transfers between devices  26 us (5%)
  matrix products  23.4 us (5%)
  loops' own time  15.9 us (3%)
  between operations  15.6 us (3%)
    psum x1, waiting for transfers between devices, per_device(): totals, target_sum = lax.psum((probe_acc, local_target), ('row', 'col'))  250 us
    psum x1, blocking collectives, per_device(): totals, target_sum = lax.psum((probe_acc, local_target), ('row', 'col'))  82.9 us
    dynamic_update_slice x4, local copies, waits for them, and re-layouts, visit(): lax.dynamic_update_slice(canvas, current + update, (anchor, offset[0], of...  34.2 us
    another operation x1, loops' own time, per_device(): lax.fori_loop(0, frame_total, visit, (canvas_start, probe_start))  15.9 us
    dot_general x8, matrix products, transform(): mixed = jnp.dot(left_matrix, stacked, precision=lax.Precision.HIGHEST)  14.9 us
    add x4, other arithmetic, visit(): current + update  12.6 us
    ppermute x4, starting transfers between devices, shifted(): return lax.ppermute(block, axis, route)  12 us
    ppermute x2, starting transfers between devices, padded(): lax.ppermute(lax.slice_in_dim(block, block.shape[dim] - width, None, axis...  10.7 us
  transfers between devices with their start and end apart: 9, of which 6 were waited for; matrix products, arithmetic and copies ran while one was open for 1% of the time, Pallas kernels for 0%

commit v1 on v0

v1 whole, which is shorter than its diff:
```python
import functools
import math

import jax
import jax.numpy as jnp
import numpy as np
from jax import lax
from jax.experimental import pallas as pl
from jax.experimental.pallas import tpu as pltpu
from jax.sharding import PartitionSpec as P

W = 256
HALF = W // 2
MARGIN = 32
FRAMES = 4
SIDE = W + 2 * MARGIN
LEAD = 2 * MARGIN

smoothing = 0.1
regular = 1.0
epsilon = 1e-06

MESH = pl.DeviceIdType.MESH
F32 = jnp.float32
BF16 = jnp.bfloat16

COMPASS = ((-1, 0), (1, 0), (0, -1), (0, 1), (-1, -1), (-1, 1), (1, -1), (1, 1))


def dft_tables():
    k = np.arange(HALF)
    j = np.arange(HALF)
    mats = []
    for parity in (0, 1):
        phase = (2 * k[:, None] + parity) * j[None, :] % W
        z = np.exp(-2j * np.pi * phase / W) / math.sqrt(W)
        mats.append(np.block([[z.real, -z.imag], [z.imag, z.real]]))
    mats += [m.T for m in mats]
    full = np.stack(mats)
    high = full.astype(BF16)
    low = (full - high.astype(np.float64)).astype(BF16)
    return np.stack([high, low], 1)


def sort_table():
    table = np.zeros((W, W), np.float32)
    k = np.arange(HALF)
    table[2 * k, k] = 1
    table[2 * k + 1, HALF + k] = 1
    return table.astype(BF16)


def split(x):
    high = x.astype(BF16)
    return high, (x - high.astype(F32)).astype(BF16)


def lanes(rows=8):
    return lax.broadcasted_iota(jnp.int32, (rows, 128), 1)


def greet(partners):
    barrier = pltpu.get_barrier_semaphore()
    for partner in partners:
        pl.semaphore_signal(barrier, inc=1, device_id=partner, device_id_type=MESH)
    pl.semaphore_wait(barrier, len(partners))


def neighbours(r, c, rows, cols):
    return [(lax.rem(r + dr + rows, rows), lax.rem(c + dc + cols, cols)) for dr, dc in COMPASS]


def pack(blocks, shift):
    group = lanes() // 32
    out = None
    for q, block in enumerate(blocks):
        amount = (shift + 32 * q) % 128
        turned = pltpu.roll(block, amount, 1) if amount else block
        out = turned if out is None else jnp.where(group == q, turned, out)
    return out


def halo_kernel(rows, cols, obj, ext, strips, from_ns, from_we, from_corner, send_sem, recv_sem):
    r, c = lax.axis_index("row"), lax.axis_index("col")
    around = neighbours(r, c, rows, cols)
    barrier = pltpu.get_barrier_semaphore()
    for partner in around:
        pl.semaphore_signal(barrier, inc=1, device_id=partner, device_id_type=MESH)
    for p in range(2):
        for j in range(8):
            left = [obj[p, pl.ds(32 * j + 8 * q, 8), 0:128] for q in range(4)]
            right = [obj[p, pl.ds(32 * j + 8 * q, 8), 128:256] for q in range(4)]
            strips[0, p, pl.ds(8 * j, 8), :] = pack(left, 0)
            strips[1, p, pl.ds(8 * j, 8), :] = pack(right, 32)
    pl.semaphore_wait(barrier, len(around))
    moves = (
        (obj.at[:, 0:32, :], from_ns.at[1]),
        (obj.at[:, W - 32 : W, :], from_ns.at[0]),
        (strips.at[0], from_we.at[1]),
        (strips.at[1], from_we.at[0]),
        (strips.at[0, :, 0:8, :], from_corner.at[3]),
        (strips.at[1, :, 0:8, :], from_corner.at[2]),
        (strips.at[0, :, 56:64, :], from_corner.at[1]),
        (strips.at[1, :, 56:64, :], from_corner.at[0]),
    )
    copies = []
    for i, (src, dst) in enumerate(moves):
        copies.append(
            pltpu.make_async_remote_copy(
                src_ref=src,
                dst_ref=dst,
                send_sem=send_sem.at[i],
                recv_sem=recv_sem.at[i],
                device_id=around[i],
                device_id_type=MESH,
            )
        )
    for i in (4, 5, 6, 7, 0, 1, 2, 3):
        copies[i].start()
    for copy in copies:
        copy.wait()
    lane = lanes()
    first = lane < 32
    second = lane < 64
    zero = jnp.zeros((8, 128), F32)
    has_n, has_s = r > 0, r < rows - 1
    has_w, has_e = c > 0, c < cols - 1

    def strip(ref, at, q, target, keep):
        amount = (target - 32 * q) % 128
        block = ref[at]
        block = pltpu.roll(block, amount, 1) if amount else block
        return jnp.where(keep, block, zero)

    def place(p, row, centre, west, east):
        t0, t1 = pltpu.roll(centre[0], 32, 1), pltpu.roll(centre[1], 32, 1)
        ext[p, 0, pl.ds(row, 8), :] = jnp.where(first, west, t0)
        ext[p, 1, pl.ds(row, 8), :] = jnp.where(first, t0, t1)
        ext[p, 2, pl.ds(row, 8), :] = jnp.where(first, t1, jnp.where(second, east, zero))

    for p in range(2):
        for k in range(4):
            for side, (keep_v, base) in enumerate(((has_n, 0), (has_s, MARGIN + W))):
                block = from_ns[side, p, pl.ds(8 * k, 8), :]
                block = jnp.where(keep_v, block, jnp.zeros_like(block))
                west = strip(from_corner, (2 * side, p, slice(0, 8)), k, 0, has_w & keep_v)
                east = strip(from_corner, (2 * side + 1, p, slice(0, 8)), k, 32, has_e & keep_v)
                place(p, base + 8 * k, (block[:, :128], block[:, 128:]), west, east)
        for j in range(8):
            for q in range(4):
                at = 32 * j + 8 * q
                block = obj[p, pl.ds(at, 8), :]
                west = strip(from_we, (0, p, pl.ds(8 * j, 8)), q, 0, has_w)
                east = strip(from_we, (1, p, pl.ds(8 * j, 8)), q, 32, has_e)
                place(p, MARGIN + at, (block[:, :128], block[:, 128:]), west, east)


def triple(left, right):
    a = jnp.concatenate([left[0], left[0], left[1]], axis=1)
    b = jnp.concatenate([right[0], right[1], right[0]], axis=0)
    return jnp.dot(a, b, preferred_element_type=F32)


STEP = 16


def frames_kernel(
    pos,
    ext,
    probe,
    amps_hbm,
    table,
    sort,
    canvas,
    acc,
    amp_sum,
    amps,
    spread,
    wave,
    win,
    sorted_amp,
    half,
    mid,
    out_mid,
    amp_sem,
):
    loads = []
    for f in range(FRAMES):
        for t in range(2):
            loads.append(
                pltpu.make_async_copy(
                    amps_hbm.at[f, :, 128 * t : 128 * t + 128], amps.at[f, t], amp_sem.at[2 * f + t]
                )
            )
            loads[-1].start()
    lane = lanes(STEP)
    zero = jnp.zeros((STEP, 128), F32)

    def clear(i, _):
        for f in range(FRAMES):
            for p in range(3):
                blank = jnp.zeros((16, 128), F32)
                for t in range(3):
                    spread[f, p, t, pl.ds(16 * i, 16), :] = blank
                    spread[f, p, t, pl.ds(LEAD + W + 16 * i, 16), :] = blank
        return 0

    lax.fori_loop(0, LEAD // 16, clear, 0)

    def clear_acc(i, _):
        for p in range(3):
            acc[p, pl.ds(32 * i, 32), :] = jnp.zeros((32, W), F32)
        return 0

    lax.fori_loop(0, W // 32, clear_acc, 0)

    sums = jnp.zeros((8, 128), F32)
    for f in range(FRAMES):
        loads[2 * f].wait()
        loads[2 * f + 1].wait()
        parts = []
        for parity in (0, 1):
            a = jnp.concatenate([amps[f, t, pl.ds(parity, HALF, stride=2), :] for t in range(2)], axis=1)
            squares = a * a
            sums = sums + (squares[:, :128] + squares[:, 128:]).reshape(16, 8, 128).sum(axis=0)
            high = a.astype(BF16)
            rest = a - high.astype(F32)
            middle = rest.astype(BF16)
            low = (rest - middle.astype(F32)).astype(BF16)
            parts.append(jnp.concatenate([high, middle, low], axis=1))
        both = jnp.concatenate(parts, axis=0)
        sorter = sort[...]
        sorted_amp[f] = jnp.dot(
            both, jnp.concatenate([sorter, sorter, sorter], axis=0), preferred_element_type=F32
        )
    amp_sum[...] = sums

    def visit(f, _):
        a = pos[2 * f]
        b = pos[2 * f + 1]
        back = lax.rem(128 - b, 128)
        keep = lane < 128 - b
        behind = lane >= b

        def gather(p, row):
            tiles = [ext[p, t, pl.ds(a + row, STEP), :] for t in range(3)]
            turned = [pltpu.roll(t, back, 1) for t in tiles]
            return jnp.concatenate(
                [jnp.where(keep, turned[0], turned[1]), jnp.where(keep, turned[1], turned[2])], axis=1
            )

        def scatter(p, row, value):
            v0, v1 = pltpu.roll(value[:, :128], b, 1), pltpu.roll(value[:, 128:], b, 1)
            at = pl.ds(LEAD + row, STEP)
            spread[f, p, 0, at, :] = jnp.where(behind, v0, zero)
            spread[f, p, 1, at, :] = jnp.where(behind, v1, v0)
            spread[f, p, 2, at, :] = jnp.where(behind, zero, v1)

        def first_step(i, _):
            at = [pl.multiple_of(STEP * i, STEP), pl.multiple_of(HALF + STEP * i, STEP)]
            waves = []
            for row in at:
                here = pl.ds(row, STEP)
                wr, wi = gather(0, row), gather(1, row)
                pr, pi = probe[0, here, :], probe[1, here, :]
                win[0, here, :] = wr
                win[1, here, :] = wi
                acc[2, here, :] += wr * wr + wi * wi
                er, ei = pr * wr - pi * wi, pr * wi + pi * wr
                wave[0, here, :] = er
                wave[1, here, :] = ei
                scatter(2, row, pr * pr + pi * pi)
                waves.append((er, ei))
            for part in range(2):
                top, low = waves[0][part], waves[1][part]
                for side, value in enumerate((top + low, top - low)):
                    h, l = split(value)
                    half[side, 0, pl.ds(HALF * part + at[0], STEP), :] = h
                    half[side, 1, pl.ds(HALF * part + at[0], STEP), :] = l
            return 0

        lax.fori_loop(0, HALF // STEP, first_step, 0)
        for side in range(2):
            mid[side] = triple((table[side, 0], table[side, 1]), (half[side, 0], half[side, 1]))

        def second_step(i, _):
            row = pl.multiple_of(STEP * i, STEP)
            for parity in range(2):
                zr = mid[parity, pl.ds(row, STEP), :]
                zi = mid[parity, pl.ds(HALF + row, STEP), :]
                here = pl.ds(HALF * parity + row, STEP)
                plus = jnp.concatenate([zr[:, :128] + zr[:, 128:], zi[:, :128] + zi[:, 128:]], axis=1)
                less = jnp.concatenate([zr[:, :128] - zr[:, 128:], zi[:, :128] - zi[:, 128:]], axis=1)
                for side, value in enumerate((plus, less)):
                    h, l = split(value)
                    half[side, 0, here, :] = h
                    half[side, 1, here, :] = l
            return 0

        lax.fori_loop(0, HALF // STEP, second_step, 0)
        for side in range(2):
            mid[side] = triple((half[side, 0], half[side, 1]), (table[2 + side, 0], table[2 + side, 1]))

        def third_step(i, _):
            here = pl.ds(pl.multiple_of(STEP * i, STEP), STEP)
            amp = sorted_amp[f, here, :]
            for side in range(2):
                z = mid[side, here, :]
                zr, zi = z[:, :128], z[:, 128:]
                factor = amp[:, 128 * side : 128 * side + 128] / jnp.sqrt(zr * zr + zi * zi + smoothing)
                h, l = split(jnp.concatenate([zr * factor, zi * factor], axis=1))
                half[side, 0, here, :] = h
                half[side, 1, here, :] = l
            return 0

        lax.fori_loop(0, W // STEP, third_step, 0)
        for side in range(2):
            out_mid[side] = triple((half[side, 0], half[side, 1]), (table[side, 0], table[side, 1]))

        def fourth_step(i, _):
            row = pl.multiple_of(STEP * i, STEP)
            for parity in range(2):
                here = pl.ds(HALF * parity + row, STEP)
                even, odd = out_mid[0, here, :], out_mid[1, here, :]
                plus, less = even + odd, even - odd
                for part in range(2):
                    value = jnp.concatenate(
                        [plus[:, 128 * part : 128 * part + 128], less[:, 128 * part : 128 * part + 128]], axis=1
                    )
                    h, l = split(value)
                    half[parity, 0, pl.ds(HALF * part + row, STEP), :] = h
                    half[parity, 1, pl.ds(HALF * part + row, STEP), :] = l
            return 0

        lax.fori_loop(0, HALF // STEP, fourth_step, 0)
        for side in range(2):
            mid[side] = triple((table[2 + side, 0], table[2 + side, 1]), (half[side, 0], half[side, 1]))

        def fifth_step(i, _):
            row = pl.multiple_of(STEP * i, STEP)
            er, orr = mid[0, pl.ds(row, STEP), :], mid[1, pl.ds(row, STEP), :]
            ei, oi = mid[0, pl.ds(HALF + row, STEP), :], mid[1, pl.ds(HALF + row, STEP), :]
            for sign, base in ((1, 0), (-1, HALF)):
                at = pl.multiple_of(base + row, STEP)
                here = pl.ds(at, STEP)
                nr, ni = (er + orr, ei + oi) if sign > 0 else (er - orr, ei - oi)
                dr, di = nr - wave[0, here, :], ni - wave[1, here, :]
                pr, pi = probe[0, here, :], probe[1, here, :]
                wr, wi = win[0, here, :], win[1, here, :]
                scatter(0, at, pr * dr + pi * di)
                scatter(1, at, pr * di - pi * dr)
                acc[0, here, :] += wr * dr + wi * di
                acc[1, here, :] += wr * di - wi * dr
            return 0

        lax.fori_loop(0, HALF // STEP, fifth_step, 0)
        return 0

    lax.fori_loop(0, FRAMES, visit, 0)

    def gather_canvas(i, _):
        row = pl.multiple_of(16 * i, 16)
        for p in range(3):
            for t in range(3):
                total = spread[0, p, t, pl.ds(LEAD - pos[0] + row, 16), :]
                for f in range(1, FRAMES):
                    total = total + spread[f, p, t, pl.ds(LEAD - pos[2 * f] + row, 16), :]
                canvas[p, t, pl.ds(row, 16), :] = total
        return 0

    lax.fori_loop(0, SIDE // 16, gather_canvas, 0)


def reduce_kernel(
    rows,
    cols,
    canvas,
    acc,
    amp,
    obj,
    probe,
    out_obj,
    out_probe,
    strips,
    bands,
    from_ns,
    from_we,
    from_corner,
    got0,
    part0,
    got1,
    part1,
    got2,
    part2,
    got3,
    gathered,
    amp0,
    amp1,
    amp2,
    amp3,
    send_edge,
    recv_edge,
    send_sem,
    recv_sem,
    send_amp,
    recv_amp,
    send_out,
    recv_out,
):
    r, c = lax.axis_index("row"), lax.axis_index("col")
    core, x, y_lo = lax.rem(c, 2), lax.rem(c // 2, 4), c // 8
    y_hi, z = lax.rem(r, 2), r // 2
    y = 2 * y_hi + y_lo

    def place(core_, x_, y_, z_):
        return (2 * z_ + y_ // 2, (lax.rem(y_, 2) * 4 + x_) * 2 + core_)

    around = neighbours(r, c, rows, cols)
    pair = place(1 - core, x, y, z)
    along_x = [place(core, lax.rem(x + d, 4), y, z) for d in range(1, 4)]
    along_y = [place(core, x, lax.rem(y + d, 4), z) for d in range(1, 4)]
    along_z = [place(core, x, y, lax.rem(z + d, 8)) for d in range(1, 8)]
    everyone = around + [pair] + along_x + along_y + along_z
    barrier = pltpu.get_barrier_semaphore()
    for partner in everyone:
        pl.semaphore_signal(barrier, inc=1, device_id=partner, device_id_type=MESH)

    lane = lanes()
    first = lane < 32
    zero = jnp.zeros((8, 128), F32)
    for p in range(3):
        for j in range(10):
            left = [canvas[p, 0, pl.ds(32 * j + 8 * q, 8), :] for q in range(4)]
            right = [canvas[p, 2, pl.ds(32 * j + 8 * q, 8), :] for q in range(4)]
            strips[0, p, pl.ds(8 * j, 8), :] = pack(left, 0)
            strips[1, p, pl.ds(8 * j, 8), :] = pack(right, 96)
        for side, base in enumerate((0, MARGIN + W)):
            for k in range(4):
                t = [pltpu.roll(canvas[p, i, pl.ds(base + 8 * k, 8), :], 96, 1) for i in range(3)]
                bands[side, p, pl.ds(8 * k, 8), 0:128] = jnp.where(lane < 96, t[0], t[1])
                bands[side, p, pl.ds(8 * k, 8), 128:256] = jnp.where(lane < 96, t[1], t[2])
    amp0[core] = amp[...]
    pl.semaphore_wait(barrier, len(everyone))

    def send(src, dst, sends, recvs, device):
        copy = pltpu.make_async_remote_copy(
            src_ref=src, dst_ref=dst, send_sem=sends, recv_sem=recvs, device_id=device, device_id_type=MESH
        )
        copy.start()
        return copy

    other = pl.ds(pl.multiple_of((1 - core) * HALF, HALF), HALF)
    mine = pl.ds(pl.multiple_of(core * HALF, HALF), HALF)
    c0 = send(acc.at[:, other, :], got0, send_sem.at[0], recv_sem.at[0], pair)
    a0 = send(amp0.at[core], amp0.at[core], send_amp.at[0], recv_amp.at[core], pair)
    moves = (
        (bands.at[0], from_ns.at[1]),
        (bands.at[1], from_ns.at[0]),
        (strips.at[0, :, 8:72, :], from_we.at[1]),
        (strips.at[1, :, 8:72, :], from_we.at[0]),
        (strips.at[0, :, 0:8, :], from_corner.at[3]),
        (strips.at[1, :, 0:8, :], from_corner.at[2]),
        (strips.at[0, :, 72:80, :], from_corner.at[1]),
        (strips.at[1, :, 72:80, :], from_corner.at[0]),
    )
    edges = [
        send(src, dst, send_edge.at[i], recv_edge.at[i], around[i]) for i, (src, dst) in enumerate(moves)
    ]

    def arrive(dst, recvs):
        pltpu.make_async_remote_copy(
            src_ref=dst, dst_ref=dst, send_sem=recvs, recv_sem=recvs, device_id=pair, device_id_type=MESH
        ).wait_recv()

    c0.wait_recv()
    for p in range(3):
        part0[p] = acc[p, mine, :] + got0[p]
    c1 = []
    for d in range(1, 4):
        to = lax.rem(x + d, 4)
        src = part0.at[:, pl.ds(pl.multiple_of(32 * to, 32), 32), :]
        c1.append(send(src, got1.at[d - 1], send_sem.at[d], recv_sem.at[d], along_x[d - 1]))
    arrive(amp0.at[1 - core], recv_amp.at[1 - core])
    amp1[x] = amp0[0] + amp0[1]
    a1 = [
        send(amp1.at[x], amp1.at[x], send_amp.at[d], recv_amp.at[2 + x], along_x[d - 1]) for d in range(1, 4)
    ]

    for e in edges:
        e.wait_recv()
    has_n, has_s = r > 0, r < rows - 1
    has_w, has_e = c > 0, c < cols - 1

    def strip(ref, at, q, target, keep):
        amount = (target - 32 * q) % 128
        block = ref[at]
        block = pltpu.roll(block, amount, 1) if amount else block
        return jnp.where(keep, block, zero)

    for j in range(8):
        for q in range(4):
            at = 32 * j + 8 * q
            totals = []
            for p in range(3):
                t = [pltpu.roll(canvas[p, i, pl.ds(MARGIN + at, 8), :], 96, 1) for i in range(3)]
                left = jnp.where(lane < 96, t[0], t[1])
                right = jnp.where(lane < 96, t[1], t[2])
                if j in (0, 7):
                    side = 0 if j == 0 else 1
                    keep_v = has_n if j == 0 else has_s
                    band = from_ns[side, p, pl.ds(8 * q, 8), :]
                    left = left + jnp.where(keep_v, band[:, :128], zero)
                    right = right + jnp.where(keep_v, band[:, 128:], zero)
                    west = strip(from_corner, (2 * side, p, slice(0, 8)), q, 0, has_w & keep_v)
                    east = strip(from_corner, (2 * side + 1, p, slice(0, 8)), q, 96, has_e & keep_v)
                    left = left + jnp.where(first, west, zero)
                    right = right + jnp.where(lane >= 96, east, zero)
                west = strip(from_we, (0, p, pl.ds(8 * j, 8)), q, 0, has_w)
                east = strip(from_we, (1, p, pl.ds(8 * j, 8)), q, 96, has_e)
                left = left + jnp.where(first, west, zero)
                right = right + jnp.where(lane >= 96, east, zero)
                totals.append((left, right))
            for s in range(2):
                scale = 1.0 / (totals[2][s] + regular)
                for p in range(2):
                    here = (p, pl.ds(at, 8), slice(128 * s, 128 * s + 128))
                    out_obj[here] = obj[here] + totals[p][s] * scale

    for d in range(1, 4):
        arrive(got1.at[d - 1], recv_sem.at[d])
    own = pl.ds(pl.multiple_of(32 * x, 32), 32)
    part1[...] = part0[:, own, :] + got1[0] + got1[1] + got1[2]
    c2 = []
    for d in range(1, 4):
        to = lax.rem(y + d, 4)
        src = part1.at[:, pl.ds(pl.multiple_of(8 * to, 8), 8), :]
        c2.append(send(src, got2.at[d - 1], send_sem.at[3 + d], recv_sem.at[3 + d], along_y[d - 1]))
    for d in range(1, 4):
        arrive(amp1.at[lax.rem(x + d, 4)], recv_amp.at[2 + lax.rem(x + d, 4)])
    amp2[y] = amp1[0] + amp1[1] + amp1[2] + amp1[3]
    a2 = [
        send(amp2.at[y], amp2.at[y], send_amp.at[3 + d], recv_amp.at[6 + y], along_y[d - 1]) for d in range(1, 4)
    ]
    for d in range(1, 4):
        arrive(got2.at[d - 1], recv_sem.at[3 + d])
    own = pl.ds(pl.multiple_of(8 * y, 8), 8)
    part2[...] = part1[:, own, :] + got2[0] + got2[1] + got2[2]

    base = lax.rem(x + y + 2 * core, 4)
    owners = [base, base + 4]
    for t in range(2):
        for d in range(8):
            here = lax.rem(owners[t] + d, 8)

            @pl.when(z == here)
            def _(t=t, d=d):
                if d == 0:
                    got3[0] = part2[:, :, 128 * t : 128 * t + 128]
                else:
                    send(
                        part2.at[:, :, 128 * t : 128 * t + 128],
                        got3.at[d],
                        send_sem.at[7 + t],
                        recv_sem.at[7 + d],
                        place(core, x, y, owners[t]),
                    )

    for d in range(1, 4):
        arrive(amp2.at[lax.rem(y + d, 4)], recv_amp.at[6 + lax.rem(y + d, 4)])
    amp3[z] = amp2[0] + amp2[1] + amp2[2] + amp2[3]
    a3 = [
        send(amp3.at[z], amp3.at[z], send_amp.at[6 + d], recv_amp.at[10 + z], along_z[d - 1]) for d in range(1, 8)
    ]
    block = pl.ds(pl.multiple_of(HALF * core + 32 * x + 8 * y, 8), 8)
    for t in range(2):
        cut = slice(128 * t, 128 * t + 128)

        @pl.when(z == owners[t])
        def _(t=t, cut=cut):
            for d in range(1, 8):
                arrive(got3.at[d], recv_sem.at[7 + d])
            total = got3[0]
            for d in range(1, 8):
                total = total + got3[d]
            scale = 1.0 / (total[2] + regular)
            for p in range(2):
                gathered[p, block, cut] = probe[p, block, cut] + total[p] * scale
            for d in range(1, 8):
                send(
                    gathered.at[:, block, cut],
                    gathered.at[:, block, cut],
                    send_out.at[d - 1],
                    recv_out.at[t],
                    along_z[d - 1],
                )

    for t in range(2):
        cut = slice(128 * t, 128 * t + 128)

        @pl.when(z != owners[t])
        def _(t=t, cut=cut):
            arrive(gathered.at[:, block, cut], recv_out.at[t])

    g1 = [
        send(gathered.at[:, block, :], gathered.at[:, block, :], send_out.at[6 + d], recv_out.at[1 + d], along_y[d - 1])
        for d in range(1, 4)
    ]
    for d in range(1, 4):
        from_y = lax.rem(y + 4 - d, 4)
        at = pl.ds(pl.multiple_of(HALF * core + 32 * x + 8 * from_y, 8), 8)
        arrive(gathered.at[:, at, :], recv_out.at[1 + d])
    block = pl.ds(pl.multiple_of(HALF * core + 32 * x, 32), 32)
    g2 = [
        send(gathered.at[:, block, :], gathered.at[:, block, :], send_out.at[9 + d], recv_out.at[4 + d], along_x[d - 1])
        for d in range(1, 4)
    ]
    for d in range(1, 4):
        from_x = lax.rem(x + 4 - d, 4)
        at = pl.ds(pl.multiple_of(HALF * core + 32 * from_x, 32), 32)
        arrive(gathered.at[:, at, :], recv_out.at[4 + d])
    g3 = send(gathered.at[:, mine, :], gathered.at[:, mine, :], send_out.at[13], recv_out.at[8], pair)
    for d in range(1, 8):
        arrive(amp3.at[lax.rem(z + d, 8)], recv_amp.at[10 + lax.rem(z + d, 8)])
    whole = amp3[0]
    for i in range(1, 8):
        whole = whole + amp3[i]
    target = jnp.sum(whole) * (1.0 / (FRAMES * rows * cols))
    arrive(gathered.at[:, other, :], recv_out.at[8])
    power = jnp.zeros((8, W), F32)
    for p in range(2):
        g = gathered[p]
        power = power + (g * g).reshape(32, 8, W).sum(axis=0)
    scale = jnp.sqrt(jnp.full((8, W), target, F32) / (jnp.sum(power) + epsilon))
    for p in range(2):
        out_probe[p] = gathered[p] * jnp.concatenate([scale] * 32, axis=0)

    for copy in [c0, a0, g3] + edges + c1 + a1 + c2 + a2 + a3 + g1 + g2:
        copy.wait_send()

    def left(src, sends):
        pltpu.make_async_remote_copy(
            src_ref=src, dst_ref=src, send_sem=sends, recv_sem=sends, device_id=pair, device_id_type=MESH
        ).wait_send()

    for t in range(2):
        cut = slice(128 * t, 128 * t + 128)

        @pl.when(z != owners[t])
        def _(t=t, cut=cut):
            left(part2.at[:, :, cut], send_sem.at[7 + t])

        @pl.when(z == owners[t])
        def _(t=t, cut=cut):
            for d in range(1, 8):
                left(part2.at[0:2, :, cut], send_out.at[d - 1])


def vmem(*shape, dtype=F32):
    return pltpu.VMEM(shape, dtype)


def per_device(rows, cols, object_field, probe, amplitudes, positions):
    in_vmem = pl.BlockSpec(memory_space=pltpu.VMEM)
    in_smem = pl.BlockSpec(memory_space=pltpu.SMEM)
    dma = pltpu.SemaphoreType.DMA
    ext = pl.pallas_call(
        functools.partial(halo_kernel, rows, cols),
        out_shape=jax.ShapeDtypeStruct((2, 3, SIDE, 128), F32),
        in_specs=[in_vmem],
        out_specs=in_vmem,
        scratch_shapes=[
            vmem(2, 2, 64, 128),
            vmem(2, 2, 32, W),
            vmem(2, 2, 64, 128),
            vmem(4, 2, 8, 128),
            dma((8,)),
            dma((8,)),
        ],
        compiler_params=pltpu.CompilerParams(collective_id=0, has_side_effects=True),
        name="halo",
    )(object_field)

    canvas, acc, amp = pl.pallas_call(
        frames_kernel,
        out_shape=(
            jax.ShapeDtypeStruct((3, 3, SIDE, 128), F32),
            jax.ShapeDtypeStruct((3, W, W), F32),
            jax.ShapeDtypeStruct((8, 128), F32),
        ),
        in_specs=[in_smem, in_vmem, in_vmem, pl.BlockSpec(memory_space=pl.ANY), in_vmem, in_vmem],
        out_specs=(in_vmem,) * 3,
        scratch_shapes=[
            vmem(FRAMES, 2, W, 128),
            vmem(FRAMES, 3, 3, LEAD + W + LEAD, 128),
            vmem(2, W, W),
            vmem(2, W, W),
            vmem(FRAMES, W, W),
            vmem(2, 2, W, W, dtype=BF16),
            vmem(2, W, W),
            vmem(2, W, W),
            dma((2 * FRAMES,)),
        ],
        compiler_params=pltpu.CompilerParams(vmem_limit_bytes=56 * 2**20),
        name="frames",
    )(
        positions.reshape(2 * FRAMES),
        ext,
        probe,
        amplitudes[0, 0],
        jnp.asarray(dft_tables()),
        jnp.asarray(sort_table()),
    )

    return pl.pallas_call(
        functools.partial(reduce_kernel, rows, cols),
        out_shape=(jax.ShapeDtypeStruct((2, W, W), F32),) * 2,
        in_specs=[in_vmem] * 5,
        out_specs=(in_vmem,) * 2,
        scratch_shapes=[
            vmem(2, 3, 80, 128),
            vmem(2, 3, 32, W),
            vmem(2, 3, 32, W),
            vmem(2, 3, 64, 128),
            vmem(4, 3, 8, 128),
            vmem(3, HALF, W),
            vmem(3, HALF, W),
            vmem(3, 3, 32, W),
            vmem(3, 32, W),
            vmem(3, 3, 8, W),
            vmem(3, 8, W),
            vmem(8, 3, 8, 128),
            vmem(2, W, W),
            vmem(2, 8, 128),
            vmem(4, 8, 128),
            vmem(4, 8, 128),
            vmem(8, 8, 128),
            dma((8,)),
            dma((8,)),
            dma((9,)),
            dma((15,)),
            dma((14,)),
            dma((18,)),
            dma((14,)),
            dma((9,)),
        ],
        compiler_params=pltpu.CompilerParams(
            collective_id=1, has_side_effects=True, vmem_limit_bytes=40 * 2**20
        ),
        name="reduce",
    )(canvas, acc, amp, object_field, probe)


def solution(mesh):
    return jax.shard_map(
        functools.partial(per_device, mesh.shape["row"], mesh.shape["col"]),
        mesh=mesh,
        in_specs=(
            P(None, "row", "col"),
            P(),
            P("row", "col", None, None, None),
            P("row", "col", None, None),
        ),
        out_specs=(P(None, "row", "col"), P()),
        check_vma=False,
    )
```

time: 519 us -> 83.9 us (0.16)
  waiting for transfers between devices: 264 us -> 0 us
  blocking collectives: 82.9 us -> 0 us
  Pallas kernels: 0 us -> 76.8 us
  other arithmetic: 41.5 us -> 0 us
  local copies, waits for them, and re-layouts: 46.3 us -> 6.15 us
  starting transfers between devices: 26 us -> 0 us
  matrix products: 23.4 us -> 0 us
  loops' own time: 15.9 us -> 0 us
  between operations: 15.6 us -> 0.7 us
    psum x1 -> x0, waiting for transfers between devices: 250 us -> none  [per_device(): totals, target_sum = lax.psum((probe_acc, local_target), ('row', 'col'))]
    psum x1 -> x0, blocking collectives: 82.9 us -> none  [per_device(): totals, target_sum = lax.psum((probe_acc, local_target), ('row', 'col'))]
    pallas_call x0 -> x3, Pallas kernels: none -> 76.8 us  [the longest x1 38.9 us: per_device(): pl.pallas_call(functools.partial(reduce_kernel, rows, cols), out_shape=(j...]
    dynamic_update_slice x4 -> x0, local copies, waits for them, and re-layouts: 34.2 us -> none  [visit(): lax.dynamic_update_slice(canvas, current + update, (anchor, offset[0], of...]
    ppermute x8 -> x0, starting transfers between devices: 25.9 us -> none  [the longest x4 12 us: shifted(): return lax.ppermute(block, axis, route)]
    dot_general x16 -> x0, matrix products: 23.4 us -> none  [the longest x8 14.9 us: transform(): mixed = jnp.dot(left_matrix, stacked, precision=lax.Precision.HIGHEST)]
    add x12 -> x0, other arithmetic: 22.1 us -> none  [the longest x4 12.6 us: visit(): current + update]
    another operation x1 -> x0, loops' own time: 15.9 us -> none  [per_device(): lax.fori_loop(0, frame_total, visit, (canvas_start, probe_start))]
  transfers between devices with their start and end apart: 9 -> 0, of which waited for: 6 -> 0; matrix products, arithmetic and copies ran while one was open for 1% -> 0% of each run, Pallas kernels for 0% -> 0%
where the time goes in v1:
time: 83.9 us; the launch traced here: 83.6 us
  Pallas kernels  76.8 us (92%)
  local copies, waits for them, and re-layouts  6.15 us (7%)
    pallas_call x1, Pallas kernels, per_device(): pl.pallas_call(functools.partial(reduce_kernel, rows, cols), out_shape=(j...  38.9 us
    pallas_call x1, Pallas kernels, per_device(): pl.pallas_call(frames_kernel, out_shape=(jax.ShapeDtypeStruct((3, 3, SIDE...  21.4 us
    pallas_call x1, Pallas kernels, per_device(): pl.pallas_call(functools.partial(halo_kernel, rows, cols), out_shape=jax....  16.5 us
    unnamed x13, local copies, waits for them, and re-layouts  5.55 us

profile of v1, /device:TPU:1, one launch (start us, length us, event | category | flops | bytes accessed | tf_op | source)
XLA Modules:
  0.0 83.6 jit_solution(1086231483155652536)
XLA Ops:
  0.6 0.8 copy.9
  1.4 0.6 reshape.7.pos
  2.0 16.5 %halo.1.ext = f32[2,3,320,128]{3,2,1,0:T(8,128)} custom-call(f32[2,256,256]{2,1,0:T(8,128)} %obj.3), custom_call_target="tpu_custom_call" | custom-call | tf_op jit(solution)/shard_map/halo/pallas_call | solution.py:666
  18.5 0.0 copy-start
  18.5 0.0 copy-start.1
  18.5 21.4 %frames.1 = (f32[3,3,320,128]{3,2,1,0:T(8,128)}, f32[3,256,256]{2,1,0:T(8,128)}, f32[8,128]{1,0:T(8,128)}) custom-call(s32[8]{0:T(128)} %reshape.7.pos, f32[2,3,320,128]{3,2,1,0:T(8,128)} %halo.1.ext, f32[2,256,256]{2,1,0:T(8,128)} %probe.3, f32[4,256,256]{2,1,0:T(8,128)} %bitcast.1, bf16[4,2,256,256]{3,2,1,0:T(8,128)(2,1)} %constant.4.clone.table, ...), custom_call_target="tpu_custom_call" | custom-call | tf_op jit(solution)/shard_map/frames/pallas_call | solution.py:683
  39.9 0.0 copy-done
  39.9 0.0 copy-done.1
  39.9 0.0 copy-start.2
  39.9 1.4 %copy-done.2 = f32[3,3,320,128]{3,2,1,0:T(8,128)S(1)} copy-done((f32[3,3,320,128]{3,2,1,0:T(8,128)S(1)}, f32[3,3,320,128]{3,2,1,0:T(8,128)}, u32[]{:S(2)}) %copy-start.2) | copy-done | bytes 1474584
  41.3 0.0 copy-start.3
  41.3 1.1 %copy-done.3 = f32[3,256,256]{2,1,0:T(8,128)S(1)} copy-done((f32[3,256,256]{2,1,0:T(8,128)S(1)}, f32[3,256,256]{2,1,0:T(8,128)}, u32[]{:S(2)}) %copy-start.3) | copy-done | bytes 786456
  42.4 0.0 copy-start.4
  42.4 0.7 copy-done.4
  43.1 38.9 %reduce.1 = (f32[2,256,256]{2,1,0:T(8,128)S(1)}, f32[2,256,256]{2,1,0:T(8,128)S(1)}) custom-call(f32[3,3,320,128]{3,2,1,0:T(8,128)S(1)} %copy-done.2, f32[3,256,256]{2,1,0:T(8,128)S(1)} %copy-done.3, f32[8,128]{1,0:T(8,128)S(1)} %copy-done.4, f32[2,256,256]{2,1,0:T(8,128)S(1)} %copy-done, f32[2,256,256]{2,1,0:T(8,128)S(1)} %copy-done.1), custom_call_target="tpu_custom_call" | custom-call | tf_op jit(solution)/shard_map/reduce/pallas_call | solution.py:714
  82.0 0.8 copy.12
  82.8 0.8 copy.13
Async XLA Ops:
  18.5 21.4 %copy-start = (f32[2,256,256]{2,1,0:T(8,128)S(1)}, f32[2,256,256]{2,1,0:T(8,128)}, u32[]{:S(2)}) copy-start(f32[2,256,256]{2,1,0:T(8,128)} %obj.3) | copy-start | bytes 1572868
  18.5 21.4 %copy-start.1 = (f32[2,256,256]{2,1,0:T(8,128)S(1)}, f32[2,256,256]{2,1,0:T(8,128)}, u32[]{:S(2)}) copy-start(f32[2,256,256]{2,1,0:T(8,128)} %probe.3) | copy-start | bytes 1572868
  39.9 1.4 %copy-start.2 = (f32[3,3,320,128]{3,2,1,0:T(8,128)S(1)}, f32[3,3,320,128]{3,2,1,0:T(8,128)}, u32[]{:S(2)}) copy-start(f32[3,3,320,128]{3,2,1,0:T(8,128)} %get-tuple-element.5.canvas) | copy-start | bytes 4423684
  41.3 1.1 %copy-start.3 = (f32[3,256,256]{2,1,0:T(8,128)S(1)}, f32[3,256,256]{2,1,0:T(8,128)}, u32[]{:S(2)}) copy-start(f32[3,256,256]{2,1,0:T(8,128)} %get-tuple-element.6.acc) | copy-start | bytes 2359300
  42.4 0.7 copy-start.4

commit v2 on v0

v2 whole, which is shorter than its diff:
```python
import functools
import math

import jax
import jax.numpy as jnp
import numpy as np
from jax import lax
from jax.experimental import pallas as pl
from jax.experimental.pallas import tpu as pltpu
from jax.sharding import PartitionSpec as P

W = 256
HALF = W // 2
MARGIN = 32
FRAMES = 4
SIDE = W + 2 * MARGIN
LEAD = 2 * MARGIN

smoothing = 0.1
regular = 1.0
epsilon = 1e-06

MESH = pl.DeviceIdType.MESH
F32 = jnp.float32
BF16 = jnp.bfloat16

COMPASS = ((-1, 0), (1, 0), (0, -1), (0, 1), (-1, -1), (-1, 1), (1, -1), (1, 1))


def dft_tables():
    k = np.arange(HALF)
    j = np.arange(HALF)
    mats = []
    for parity in (0, 1):
        phase = (2 * k[:, None] + parity) * j[None, :] % W
        z = np.exp(-2j * np.pi * phase / W) / math.sqrt(W)
        mats.append(np.block([[z.real, -z.imag], [z.imag, z.real]]))
    mats += [m.T for m in mats]
    full = np.stack(mats)
    high = full.astype(BF16)
    low = (full - high.astype(np.float64)).astype(BF16)
    return np.stack([high, low], 1)


def sort_table():
    table = np.zeros((W, W), np.float32)
    k = np.arange(HALF)
    table[2 * k, k] = 1
    table[2 * k + 1, HALF + k] = 1
    return table.astype(BF16)


def split(x):
    high = x.astype(BF16)
    return high, (x - high.astype(F32)).astype(BF16)


def lanes(rows=8):
    return lax.broadcasted_iota(jnp.int32, (rows, 128), 1)


def neighbours(r, c, rows, cols):
    return [(lax.rem(r + dr + rows, rows), lax.rem(c + dc + cols, cols)) for dr, dc in COMPASS]


def pack(blocks, shift):
    group = lanes() // 32
    out = None
    for q, block in enumerate(blocks):
        amount = (shift + 32 * q) % 128
        turned = pltpu.roll(block, amount, 1) if amount else block
        out = turned if out is None else jnp.where(group == q, turned, out)
    return out


STEP = 16


def triple(left, right):
    a = jnp.concatenate([left[0], left[0], left[1]], axis=1)
    b = jnp.concatenate([right[0], right[1], right[0]], axis=0)
    return jnp.dot(a, b, preferred_element_type=F32)


def send(src, dst, sends, recvs, device):
    copy = pltpu.make_async_remote_copy(
        src_ref=src, dst_ref=dst, send_sem=sends, recv_sem=recvs, device_id=device, device_id_type=MESH
    )
    copy.start()
    return copy


def kernel(
    rows,
    cols,
    pos,
    obj_hbm,
    probe_hbm,
    amps_hbm,
    table_hbm,
    sort_hbm,
    out_obj,
    out_probe,
    obj,
    probe,
    amps,
    table,
    sort,
    halo_strips,
    halo_ns,
    halo_we,
    halo_corner,
    ext,
    spread,
    win,
    sorted_amp,
    half,
    mid,
    acc,
    power2,
    canvas,
    strips,
    bands,
    from_ns,
    from_we,
    from_corner,
    early0,
    early0_got,
    early1,
    early1_got,
    early2,
    got0,
    part0,
    got1,
    all2,
    gathered,
    load_sem,
    amp_sem,
    send_halo,
    recv_halo,
    send_edge,
    recv_edge,
    send_pair,
    recv_pair,
    send_e1,
    recv_e1,
    send_e2,
    recv_e2,
    send_m1,
    recv_m1,
    send_m2,
    recv_m2,
    send_ag,
    recv_ag,
    send_fw,
    recv_fw,
):
    loads = [
        pltpu.make_async_copy(src, dst, load_sem.at[i])
        for i, (src, dst) in enumerate(((obj_hbm, obj), (probe_hbm, probe), (sort_hbm, sort), (table_hbm, table)))
    ]
    loads[0].start()
    amp_loads = []
    for f in range(FRAMES):
        for t in range(2):
            amp_loads.append(
                pltpu.make_async_copy(
                    amps_hbm.at[0, 0, f, :, 128 * t : 128 * t + 128], amps.at[f, t], amp_sem.at[2 * f + t]
                )
            )

    r, c = lax.axis_index("row"), lax.axis_index("col")
    core, x, y_lo = lax.rem(c, 2), lax.rem(c // 2, 4), c // 8
    y_hi, z = lax.rem(r, 2), r // 2
    y = 2 * y_hi + y_lo

    def place(core_, x_, y_, z_):
        return (2 * z_ + y_ // 2, (lax.rem(y_, 2) * 4 + x_) * 2 + core_)

    around = neighbours(r, c, rows, cols)
    pair = place(1 - core, x, y, z)
    steps_xy = [(2, 2), (1, 2), (3, 2), (2, 1), (2, 3), (1, 1), (1, 3), (3, 1), (3, 3), (2, 0), (0, 2), (1, 0), (3, 0), (0, 1), (0, 3)]
    on_plane = [(lax.rem(x + dx, 4), lax.rem(y + dy, 4)) for dx, dy in steps_xy]
    behind_plane = [(lax.rem(x + 4 - dx, 4), lax.rem(y + 4 - dy, 4)) for dx, dy in steps_xy]
    plane = [place(core, x_, y_, z) for x_, y_ in on_plane]
    steps_z = [4, 3, 5, 2, 6, 1, 7]
    column = [place(core, x, y, lax.rem(z + d, 8)) for d in steps_z]
    everyone = around + [pair] + plane + column
    barrier = pltpu.get_barrier_semaphore()
    for partner in everyone:
        pl.semaphore_signal(barrier, inc=1, device_id=partner, device_id_type=MESH)
    loads[1].start()
    loads[2].start()
    for load in amp_loads:
        load.start()
    loads[3].start()

    loads[0].wait()
    for p in range(2):
        for j in range(8):
            left = [obj[p, pl.ds(32 * j + 8 * q, 8), 0:128] for q in range(4)]
            right = [obj[p, pl.ds(32 * j + 8 * q, 8), 128:256] for q in range(4)]
            halo_strips[0, p, pl.ds(8 * j, 8), :] = pack(left, 0)
            halo_strips[1, p, pl.ds(8 * j, 8), :] = pack(right, 32)
    pl.semaphore_wait(barrier, len(everyone))
    moves = (
        (obj.at[:, 0:32, :], halo_ns.at[1]),
        (obj.at[:, W - 32 : W, :], halo_ns.at[0]),
        (halo_strips.at[0], halo_we.at[1]),
        (halo_strips.at[1], halo_we.at[0]),
        (halo_strips.at[0, :, 0:8, :], halo_corner.at[3]),
        (halo_strips.at[1, :, 0:8, :], halo_corner.at[2]),
        (halo_strips.at[0, :, 56:64, :], halo_corner.at[1]),
        (halo_strips.at[1, :, 56:64, :], halo_corner.at[0]),
    )
    halo = [
        send(moves[i][0], moves[i][1], send_halo.at[i], recv_halo.at[i], around[i]) for i in (4, 5, 6, 7, 0, 1, 2, 3)
    ]

    lane = lanes(STEP)
    zero = jnp.zeros((STEP, 128), F32)

    def clear(i, _):
        for f in range(FRAMES):
            for p in range(3):
                for t in range(3):
                    spread[f, p, t, pl.ds(16 * i, 16), :] = zero
                    spread[f, p, t, pl.ds(LEAD + W + 16 * i, 16), :] = zero
        return 0

    lax.fori_loop(0, LEAD // 16, clear, 0)
    loads[1].wait()
    loads[2].wait()
    sums = jnp.zeros((8, 128), F32)
    for f in range(FRAMES):
        amp_loads[2 * f].wait()
        amp_loads[2 * f + 1].wait()
        parts = []
        for parity in (0, 1):
            a = jnp.concatenate([amps[f, t, pl.ds(parity, HALF, stride=2), :] for t in range(2)], axis=1)
            squares = a * a
            sums = sums + (squares[:, :128] + squares[:, 128:]).reshape(16, 8, 128).sum(axis=0)
            high = a.astype(BF16)
            rest = a - high.astype(F32)
            middle = rest.astype(BF16)
            low = (rest - middle.astype(F32)).astype(BF16)
            parts.append(jnp.concatenate([high, middle, low], axis=1))
        both = jnp.concatenate(parts, axis=0)
        sorter = sort[...]
        sorted_amp[f] = jnp.dot(
            both, jnp.concatenate([sorter, sorter, sorter], axis=0), preferred_element_type=F32
        )
    early0[pl.ds(W, 8), :] = sums

    at_row = [pos[0, 0, 0, f] for f in range(FRAMES)]
    at_col = [pos[0, 0, 1, f] for f in range(FRAMES)]

    def gather(f, p, row):
        b = at_col[f]
        tiles = [ext[p, t, pl.ds(at_row[f] + row, STEP), :] for t in range(3)]
        turned = [pltpu.roll(t, lax.rem(128 - b, 128), 1) for t in tiles]
        keep = lane < 128 - b
        return jnp.concatenate(
            [jnp.where(keep, turned[0], turned[1]), jnp.where(keep, turned[1], turned[2])], axis=1
        )

    def scatter(f, p, row, value):
        b = at_col[f]
        behind = lane >= b
        v0, v1 = pltpu.roll(value[:, :128], b, 1), pltpu.roll(value[:, 128:], b, 1)
        at = pl.ds(LEAD + row, STEP)
        spread[f, p, 0, at, :] = jnp.where(behind, v0, zero)
        spread[f, p, 1, at, :] = jnp.where(behind, v1, v0)
        spread[f, p, 2, at, :] = jnp.where(behind, zero, v1)

    for row in range(0, W, STEP):
        here = pl.ds(row, STEP)
        pr, pi = probe[0, here, :], probe[1, here, :]
        for f in range(FRAMES):
            scatter(f, 2, row, pr * pr + pi * pi)

    def gather_canvas(planes):
        def some(i, _):
            row = pl.multiple_of(16 * i, 16)
            for p in planes:
                for t in range(3):
                    total = spread[0, p, t, pl.ds(LEAD - at_row[0] + row, 16), :]
                    for f in range(1, FRAMES):
                        total = total + spread[f, p, t, pl.ds(LEAD - at_row[f] + row, 16), :]
                    canvas[p, t, pl.ds(row, 16), :] = total
            return 0

        lax.fori_loop(0, SIDE // 16, some, 0)

    gather_canvas((2,))
    loads[3].wait()

    lane8 = lanes()
    first = lane8 < 32
    second = lane8 < 64
    zero8 = jnp.zeros((8, 128), F32)
    has_n, has_s = r > 0, r < rows - 1
    has_w, has_e = c > 0, c < cols - 1

    def strip(ref, at, q, target, keep):
        amount = (target - 32 * q) % 128
        block = ref[at]
        block = pltpu.roll(block, amount, 1) if amount else block
        return jnp.where(keep, block, zero8)

    def put(p, row, centre, west, east):
        t0, t1 = pltpu.roll(centre[0], 32, 1), pltpu.roll(centre[1], 32, 1)
        ext[p, 0, pl.ds(row, 8), :] = jnp.where(first, west, t0)
        ext[p, 1, pl.ds(row, 8), :] = jnp.where(first, t0, t1)
        ext[p, 2, pl.ds(row, 8), :] = jnp.where(first, t1, jnp.where(second, east, zero8))

    for copy in halo:
        copy.wait_recv()
    for p in range(2):
        for k in range(4):
            for side, (keep_v, base) in enumerate(((has_n, 0), (has_s, MARGIN + W))):
                block = halo_ns[side, p, pl.ds(8 * k, 8), :]
                block = jnp.where(keep_v, block, jnp.zeros_like(block))
                west = strip(halo_corner, (2 * side, p, slice(0, 8)), k, 0, has_w & keep_v)
                east = strip(halo_corner, (2 * side + 1, p, slice(0, 8)), k, 32, has_e & keep_v)
                put(p, base + 8 * k, (block[:, :128], block[:, 128:]), west, east)
        for j in range(8):
            for q in range(4):
                at = 32 * j + 8 * q
                block = obj[p, pl.ds(at, 8), :]
                west = strip(halo_we, (0, p, pl.ds(8 * j, 8)), q, 0, has_w)
                east = strip(halo_we, (1, p, pl.ds(8 * j, 8)), q, 32, has_e)
                put(p, MARGIN + at, (block[:, :128], block[:, 128:]), west, east)

    def halve(f, stage, side, rows_at, value):
        h, l = split(value)
        half[f, stage, side, 0, rows_at, :] = h
        half[f, stage, side, 1, rows_at, :] = l

    for row in range(0, HALF, STEP):
        sums = [jnp.zeros((STEP, W), F32)] * 2
        for f in range(FRAMES):
            waves = []
            for i, base in enumerate((row, HALF + row)):
                here = pl.ds(base, STEP)
                wr, wi = gather(f, 0, base), gather(f, 1, base)
                pr, pi = probe[0, here, :], probe[1, here, :]
                win[f, 0, here, :] = wr
                win[f, 1, here, :] = wi
                sums[i] = sums[i] + (wr * wr + wi * wi)
                waves.append((pr * wr - pi * wi, pr * wi + pi * wr))
            for part in range(2):
                top, low = waves[0][part], waves[1][part]
                where = pl.ds(HALF * part + row, STEP)
                halve(f, 0, 0, where, top + low)
                halve(f, 0, 1, where, top - low)
        for i, base in enumerate((row, HALF + row)):
            power2[pl.ds(base, STEP), :] = sums[i][:, :128]
            power2[pl.ds(W + base, STEP), :] = sums[i][:, 128:]

    mine8 = pl.multiple_of(core * HALF, HALF)
    other8 = pl.multiple_of((1 - core) * HALF, HALF)
    for t in range(2):
        early0[pl.ds(HALF * t, HALF), :] = power2[pl.ds(W * t + other8, HALF), :]
    e0 = send(early0, early0_got, send_pair.at[0], recv_pair.at[0], pair)

    def left_dots(stage, flip):
        for f in range(FRAMES):
            for side in range(2):
                mid[f, stage, side] = triple(
                    (table[flip + side, 0], table[flip + side, 1]),
                    (half[f, stage, side, 0], half[f, stage, side, 1]),
                )

    def right_dots(stage, flip):
        for f in range(FRAMES):
            for side in range(2):
                mid[f, stage, side] = triple(
                    (half[f, stage, side, 0], half[f, stage, side, 1]),
                    (table[flip + side, 0], table[flip + side, 1]),
                )

    left_dots(0, 0)
    for f in range(FRAMES):
        for parity in range(2):
            for row in range(0, HALF, STEP):
                zr = mid[f, 0, parity, pl.ds(row, STEP), :]
                zi = mid[f, 0, parity, pl.ds(HALF + row, STEP), :]
                here = pl.ds(HALF * parity + row, STEP)
                plus = jnp.concatenate([zr[:, :128] + zr[:, 128:], zi[:, :128] + zi[:, 128:]], axis=1)
                less = jnp.concatenate([zr[:, :128] - zr[:, 128:], zi[:, :128] - zi[:, 128:]], axis=1)
                halve(f, 1, 0, here, plus)
                halve(f, 1, 1, here, less)

    k = 4 * x + y
    e0.wait_recv()
    for i in range(16):
        for t in range(2):
            at = mine8 + 8 * i
            early1[i, pl.ds(8 * t, 8), :] = (
                power2[pl.ds(W * t + at, 8), :] + early0_got[pl.ds(HALF * t + 8 * i, 8), :]
            )
        early1[i, pl.ds(16, 8), :] = early0[pl.ds(W, 8), :] + early0_got[pl.ds(W, 8), :]
    early1_got[k] = early1[k]
    e1 = []
    for i, (x_, y_) in enumerate(on_plane):
        e1.append(send(early1.at[4 * x_ + y_], early1_got.at[k], send_e1.at[i], recv_e1.at[k], plane[i]))

    right_dots(1, 2)
    for f in range(FRAMES):
        for side in range(2):
            for row in range(0, W, STEP):
                here = pl.ds(row, STEP)
                amp = sorted_amp[f, here, 128 * side : 128 * side + 128]
                v = mid[f, 1, side, here, :]
                zr, zi = v[:, :128], v[:, 128:]
                factor = amp * lax.rsqrt(zr * zr + zi * zi + smoothing)
                halve(f, 2, side, here, jnp.concatenate([zr * factor, zi * factor], axis=1))

    right_dots(2, 0)

    def arrive(dst, recvs):
        pltpu.make_async_remote_copy(
            src_ref=dst, dst_ref=dst, send_sem=recvs, recv_sem=recvs, device_id=pair, device_id_type=MESH
        ).wait_recv()

    for x_, y_ in behind_plane:
        arrive(early1_got.at[4 * x_ + y_], recv_e1.at[4 * x_ + y_])
    total = early1_got[0]
    for i in range(1, 16):
        total = total + early1_got[i]
    early2[z] = total
    e2 = [send(early2.at[z], early2.at[z], send_e2.at[i], recv_e2.at[z], column[i]) for i in range(7)]

    for f in range(FRAMES):
        for parity in range(2):
            for row in range(0, HALF, STEP):
                here = pl.ds(HALF * parity + row, STEP)
                even, odd = mid[f, 2, 0, here, :], mid[f, 2, 1, here, :]
                plus, less = even + odd, even - odd
                for part in range(2):
                    cut = slice(128 * part, 128 * part + 128)
                    value = jnp.concatenate([plus[:, cut], less[:, cut]], axis=1)
                    halve(f, 3, parity, pl.ds(HALF * part + row, STEP), value)

    left_dots(3, 2)
    for row in range(0, HALF, STEP):
        parts = []
        for f in range(FRAMES):
            er, orr = mid[f, 3, 0, pl.ds(row, STEP), :], mid[f, 3, 1, pl.ds(row, STEP), :]
            ei, oi = mid[f, 3, 0, pl.ds(HALF + row, STEP), :], mid[f, 3, 1, pl.ds(HALF + row, STEP), :]
            parts.append(((er + orr, ei + oi), (er - orr, ei - oi)))
        for side, base in enumerate((row, HALF + row)):
            here = pl.ds(base, STEP)
            pr, pi = probe[0, here, :], probe[1, here, :]
            sums = [jnp.zeros((STEP, W), F32)] * 2
            for f in range(FRAMES):
                wr, wi = win[f, 0, here, :], win[f, 1, here, :]
                dr = parts[f][side][0] - (pr * wr - pi * wi)
                di = parts[f][side][1] - (pr * wi + pi * wr)
                scatter(f, 0, base, pr * dr + pi * di)
                scatter(f, 1, base, pr * di - pi * dr)
                sums = [sums[0] + (wr * dr + wi * di), sums[1] + (wr * di - wi * dr)]
            acc[0, here, :], acc[1, here, :] = sums

    mine = pl.ds(mine8, HALF)
    other = pl.ds(other8, HALF)
    c0 = send(acc.at[:, other, :], got0, send_pair.at[1], recv_pair.at[1], pair)

    gather_canvas((0, 1))
    for p in range(3):
        for side, base in enumerate((0, MARGIN + W)):
            for q in range(4):
                t = [pltpu.roll(canvas[p, i, pl.ds(base + 8 * q, 8), :], 96, 1) for i in range(3)]
                bands[side, p, pl.ds(8 * q, 8), 0:128] = jnp.where(lane8 < 96, t[0], t[1])
                bands[side, p, pl.ds(8 * q, 8), 128:256] = jnp.where(lane8 < 96, t[1], t[2])

    c0.wait_recv()
    for p in range(2):
        part0[p] = acc[p, mine, :] + got0[p]
    c1 = []
    for i, (x_, y_) in enumerate(on_plane):
        src = part0.at[:, pl.ds(pl.multiple_of(8 * (4 * x_ + y_), 8), 8), :]
        c1.append(send(src, got1.at[i], send_m1.at[i], recv_m1.at[i], plane[i]))

    for p in range(3):
        for j in range(10):
            left = [canvas[p, 0, pl.ds(32 * j + 8 * q, 8), :] for q in range(4)]
            right = [canvas[p, 2, pl.ds(32 * j + 8 * q, 8), :] for q in range(4)]
            strips[0, p, pl.ds(8 * j, 8), :] = pack(left, 0)
            strips[1, p, pl.ds(8 * j, 8), :] = pack(right, 96)

    own = pl.ds(pl.multiple_of(8 * k, 8), 8)
    for copy in c1:
        copy.wait_recv()
    total = part0[:, own, :]
    for i in range(15):
        total = total + got1[i]
    all2[z] = total
    c2 = [send(all2.at[z], all2.at[z], send_m2.at[i], recv_m2.at[z], column[i]) for i in range(7)]

    moves = (
        (bands.at[0], from_ns.at[1]),
        (bands.at[1], from_ns.at[0]),
        (strips.at[0, :, 8:72, :], from_we.at[1]),
        (strips.at[1, :, 8:72, :], from_we.at[0]),
        (strips.at[0, :, 0:8, :], from_corner.at[3]),
        (strips.at[1, :, 0:8, :], from_corner.at[2]),
        (strips.at[0, :, 72:80, :], from_corner.at[1]),
        (strips.at[1, :, 72:80, :], from_corner.at[0]),
    )
    edges = [
        send(moves[i][0], moves[i][1], send_edge.at[i], recv_edge.at[i], around[i]) for i in (4, 5, 6, 7, 0, 1, 2, 3)
    ]

    for d in range(1, 8):
        arrive(early2.at[lax.rem(z + d, 8)], recv_e2.at[lax.rem(z + d, 8)])
    total = early2[0]
    for i in range(1, 8):
        total = total + early2[i]
    weight = 1.0 / (jnp.concatenate([total[0:8], total[8:16]], axis=1) + regular)
    target = jnp.sum(total[16:24]) * (1.0 / (FRAMES * rows * cols))

    block = pl.ds(pl.multiple_of(HALF * core + 8 * k, 8), 8)
    for d in range(1, 8):
        arrive(all2.at[lax.rem(z + d, 8)], recv_m2.at[lax.rem(z + d, 8)])
    total = all2[0]
    for i in range(1, 8):
        total = total + all2[i]
    for p in range(2):
        gathered[p, block, :] = probe[p, block, :] + total[p] * weight
    g1 = [
        send(gathered.at[:, block, :], gathered.at[:, block, :], send_ag.at[i], recv_ag.at[i], plane[i])
        for i in range(15)
    ]
    fw = [send(gathered.at[:, block, :], gathered.at[:, block, :], send_fw.at[15], recv_fw.at[15], pair)]

    for copy in edges:
        copy.wait_recv()
    for j in range(8):
        for q in range(4):
            at = 32 * j + 8 * q
            totals = []
            for p in range(3):
                t = [pltpu.roll(canvas[p, i, pl.ds(MARGIN + at, 8), :], 96, 1) for i in range(3)]
                left = jnp.where(lane8 < 96, t[0], t[1])
                right = jnp.where(lane8 < 96, t[1], t[2])
                if j in (0, 7):
                    side = 0 if j == 0 else 1
                    keep_v = has_n if j == 0 else has_s
                    band = from_ns[side, p, pl.ds(8 * q, 8), :]
                    left = left + jnp.where(keep_v, band[:, :128], zero8)
                    right = right + jnp.where(keep_v, band[:, 128:], zero8)
                    west = strip(from_corner, (2 * side, p, slice(0, 8)), q, 0, has_w & keep_v)
                    east = strip(from_corner, (2 * side + 1, p, slice(0, 8)), q, 96, has_e & keep_v)
                    left = left + jnp.where(first, west, zero8)
                    right = right + jnp.where(lane8 >= 96, east, zero8)
                west = strip(from_we, (0, p, pl.ds(8 * j, 8)), q, 0, has_w)
                east = strip(from_we, (1, p, pl.ds(8 * j, 8)), q, 96, has_e)
                left = left + jnp.where(first, west, zero8)
                right = right + jnp.where(lane8 >= 96, east, zero8)
                totals.append((left, right))
            for s in range(2):
                scale = 1.0 / (totals[2][s] + regular)
                for p in range(2):
                    here = (p, pl.ds(at, 8), slice(128 * s, 128 * s + 128))
                    out_obj[here] = obj[here] + totals[p][s] * scale

    for i in reversed(range(15)):
        x_, y_ = behind_plane[i]
        at = pl.ds(pl.multiple_of(HALF * core + 8 * (4 * x_ + y_), 8), 8)
        arrive(gathered.at[:, at, :], recv_ag.at[i])
        fw.append(send(gathered.at[:, at, :], gathered.at[:, at, :], send_fw.at[i], recv_fw.at[i], pair))
    for i in range(16):
        x_, y_ = behind_plane[i] if i < 15 else (x, y)
        at = pl.ds(pl.multiple_of(HALF * (1 - core) + 8 * (4 * x_ + y_), 8), 8)
        arrive(gathered.at[:, at, :], recv_fw.at[i])
    power = jnp.zeros((8, W), F32)
    for p in range(2):
        g = gathered[p]
        power = power + (g * g).reshape(32, 8, W).sum(axis=0)
    scale = jnp.sqrt(jnp.full((8, W), target, F32) / (jnp.sum(power) + epsilon))
    for p in range(2):
        out_probe[p] = gathered[p] * jnp.concatenate([scale] * 32, axis=0)

    for copy in halo + [e0, c0] + e1 + e2 + c1 + c2 + edges + g1 + fw:
        copy.wait_send()


def vmem(*shape, dtype=F32):
    return pltpu.VMEM(shape, dtype)


def per_device(rows, cols, object_field, probe, amplitudes, positions):
    in_vmem = pl.BlockSpec(memory_space=pltpu.VMEM)
    in_smem = pl.BlockSpec(memory_space=pltpu.SMEM)
    in_hbm = pl.BlockSpec(memory_space=pl.ANY)
    dma = pltpu.SemaphoreType.DMA
    return pl.pallas_call(
        functools.partial(kernel, rows, cols),
        out_shape=(jax.ShapeDtypeStruct((2, W, W), F32),) * 2,
        in_specs=[in_smem] + [in_hbm] * 5,
        out_specs=(in_vmem,) * 2,
        scratch_shapes=[
            vmem(2, W, W),
            vmem(2, W, W),
            vmem(FRAMES, 2, W, 128),
            vmem(4, 2, W, W, dtype=BF16),
            vmem(W, W, dtype=BF16),
            vmem(2, 2, 64, 128),
            vmem(2, 2, 32, W),
            vmem(2, 2, 64, 128),
            vmem(4, 2, 8, 128),
            vmem(2, 3, SIDE, 128),
            vmem(FRAMES, 3, 3, LEAD + W + LEAD, 128),
            vmem(FRAMES, 2, W, W),
            vmem(FRAMES, W, W),
            vmem(FRAMES, 4, 2, 2, W, W, dtype=BF16),
            vmem(FRAMES, 4, 2, W, W),
            vmem(2, W, W),
            vmem(2 * W, 128),
            vmem(3, 3, SIDE, 128),
            vmem(2, 3, 80, 128),
            vmem(2, 3, 32, W),
            vmem(2, 3, 32, W),
            vmem(2, 3, 64, 128),
            vmem(4, 3, 8, 128),
            vmem(W + 8, 128),
            vmem(W + 8, 128),
            vmem(16, 24, 128),
            vmem(16, 24, 128),
            vmem(8, 24, 128),
            vmem(2, HALF, W),
            vmem(2, HALF, W),
            vmem(15, 2, 8, W),
            vmem(8, 2, 8, W),
            vmem(2, W, W),
            dma((4,)),
            dma((2 * FRAMES,)),
            dma((8,)),
            dma((8,)),
            dma((8,)),
            dma((8,)),
            dma((2,)),
            dma((2,)),
            dma((15,)),
            dma((16,)),
            dma((7,)),
            dma((8,)),
            dma((15,)),
            dma((15,)),
            dma((7,)),
            dma((8,)),
            dma((15,)),
            dma((15,)),
            dma((16,)),
            dma((16,)),
        ],
        compiler_params=pltpu.CompilerParams(
            collective_id=0, has_side_effects=True, vmem_limit_bytes=56 * 2**20
        ),
        name="ptycho",
    )(
        jnp.swapaxes(positions, 2, 3),
        object_field,
        probe,
        amplitudes,
        jnp.asarray(dft_tables()),
        jnp.asarray(sort_table()),
    )


def solution(mesh):
    return jax.shard_map(
        functools.partial(per_device, mesh.shape["row"], mesh.shape["col"]),
        mesh=mesh,
        in_specs=(
            P(None, "row", "col"),
            P(),
            P("row", "col", None, None, None),
            P("row", "col", None, None),
        ),
        out_specs=(P(None, "row", "col"), P()),
        check_vma=False,
    )
```

time: 519 us -> 54.7 us (0.11)
  waiting for transfers between devices: 264 us -> 0 us
  blocking collectives: 82.9 us -> 0 us
  Pallas kernels: 0 us -> 51.2 us
  local copies, waits for them, and re-layouts: 46.3 us -> 2.72 us
  other arithmetic: 41.5 us -> 0 us
  starting transfers between devices: 26 us -> 0 us
  matrix products: 23.4 us -> 0 us
  loops' own time: 15.9 us -> 0 us
  between operations: 15.6 us -> 0.65 us
    psum x1 -> x0, waiting for transfers between devices: 250 us -> none  [per_device(): totals, target_sum = lax.psum((probe_acc, local_target), ('row', 'col'))]
    psum x1 -> x0, blocking collectives: 82.9 us -> none  [per_device(): totals, target_sum = lax.psum((probe_acc, local_target), ('row', 'col'))]
    pallas_call x0 -> x1, Pallas kernels: none -> 51.2 us  [per_device(): pl.pallas_call(functools.partial(kernel, rows, cols), out_shape=(jax.Shap...]
    dynamic_update_slice x4 -> x0, local copies, waits for them, and re-layouts: 34.2 us -> none  [visit(): lax.dynamic_update_slice(canvas, current + update, (anchor, offset[0], of...]
    ppermute x8 -> x0, starting transfers between devices: 25.9 us -> none  [the longest x4 12 us: shifted(): return lax.ppermute(block, axis, route)]
    dot_general x16 -> x0, matrix products: 23.4 us -> none  [the longest x8 14.9 us: transform(): mixed = jnp.dot(left_matrix, stacked, precision=lax.Precision.HIGHEST)]
    add x12 -> x0, other arithmetic: 22.1 us -> none  [the longest x4 12.6 us: visit(): current + update]
    another operation x1 -> x0, loops' own time: 15.9 us -> none  [per_device(): lax.fori_loop(0, frame_total, visit, (canvas_start, probe_start))]
  transfers between devices with their start and end apart: 9 -> 0, of which waited for: 6 -> 0; matrix products, arithmetic and copies ran while one was open for 1% -> 0% of each run, Pallas kernels for 0% -> 0%
where the time goes in v2:
time: 54.7 us; the launch traced here: 54.6 us
  Pallas kernels  51.2 us (94%)
  local copies, waits for them, and re-layouts  2.72 us (5%)
  between operations  0.65 us (1%)
    pallas_call x1, Pallas kernels, per_device(): pl.pallas_call(functools.partial(kernel, rows, cols), out_shape=(jax.Shap...  51.2 us
    unnamed x4, local copies, waits for them, and re-layouts  2.72 us

profile of v2, /device:TPU:1, one launch (start us, length us, event | category | flops | bytes accessed | tf_op | source)
XLA Modules:
  0.0 54.6 jit_solution(10422437594144798339)
XLA Ops:
  0.6 51.2 %ptycho.1 = (f32[2,256,256]{2,1,0:T(8,128)}, f32[2,256,256]{2,1,0:T(8,128)}) custom-call(s32[1,1,2,4]{3,2,1,0:T(2,128)} %bitcast.1, f32[2,256,256]{2,1,0:T(8,128)} %obj_hbm.1, f32[2,256,256]{2,1,0:T(8,128)} %probe_hbm.1, f32[1,1,4,256,256]{4,3,2,1,0:T(8,128)} %amps_hbm.1, bf16[4,2,256,256]{3,2,1,0:T(8,128)(2,1)} %constant.4.clone.table_hbm, ...), custom_call_target="tpu_custom_call" | custom-call | tf_op jit(solution)/shard_map/ptycho/pallas_call | solution.py:599
  51.9 0.0 copy-start
  51.9 1.9 %copy.10 = f32[2,256,256]{2,1,0:T(8,128)} copy(f32[2,256,256]{2,1,0:T(8,128)} %get-tuple-element.4) | data formatting | bytes 1048576
  53.8 0.0 copy-done
  53.8 0.8 %copy.11 = f32[2,256,256]{2,1,0:T(8,128)} copy(f32[2,256,256]{2,1,0:T(8,128)S(1)} %copy-done) | data formatting | bytes 1048576
Async XLA Ops:
  51.9 1.9 %copy-start = (f32[2,256,256]{2,1,0:T(8,128)S(1)}, f32[2,256,256]{2,1,0:T(8,128)}, u32[]{:S(2)}) copy-start(f32[2,256,256]{2,1,0:T(8,128)} %get-tuple-element.5) | copy-start | bytes 1572868

commit v3 on v2

--- a/solution.py
+++ b/solution.py
@@ -93,7 +93,7 @@
 def kernel(
     rows,
     cols,
-    pos,
+    pos_hbm,
     obj_hbm,
     probe_hbm,
     amps_hbm,
@@ -101,6 +101,7 @@
     sort_hbm,
     out_obj,
     out_probe,
+    pos,
     obj,
     probe,
     amps,
@@ -157,7 +158,9 @@
 ):
     loads = [
         pltpu.make_async_copy(src, dst, load_sem.at[i])
-        for i, (src, dst) in enumerate(((obj_hbm, obj), (probe_hbm, probe), (sort_hbm, sort), (table_hbm, table)))
+        for i, (src, dst) in enumerate(
+            ((obj_hbm, obj), (probe_hbm, probe), (sort_hbm, sort), (table_hbm, table), (pos_hbm, pos))
+        )
     ]
     loads[0].start()
     amp_loads = []
@@ -190,6 +193,7 @@
     for partner in everyone:
         pl.semaphore_signal(barrier, inc=1, device_id=partner, device_id_type=MESH)
     loads[1].start()
+    loads[4].start()
     loads[2].start()
     for load in amp_loads:
         load.start()
@@ -230,6 +234,7 @@
 
     lax.fori_loop(0, LEAD // 16, clear, 0)
     loads[1].wait()
+    loads[4].wait()
     loads[2].wait()
     sums = jnp.zeros((8, 128), F32)
     for f in range(FRAMES):
@@ -292,9 +297,6 @@
 
         lax.fori_loop(0, SIDE // 16, some, 0)
 
-    gather_canvas((2,))
-    loads[3].wait()
-
     lane8 = lanes()
     first = lane8 < 32
     second = lane8 < 64
@@ -307,6 +309,40 @@
         block = ref[at]
         block = pltpu.roll(block, amount, 1) if amount else block
         return jnp.where(keep, block, zero8)
+
+    def pack_edges(planes):
+        for p in planes:
+            for side, base in enumerate((0, MARGIN + W)):
+                for q in range(4):
+                    t = [pltpu.roll(canvas[p, i, pl.ds(base + 8 * q, 8), :], 96, 1) for i in range(3)]
+                    bands[side, p, pl.ds(8 * q, 8), 0:128] = jnp.where(lane8 < 96, t[0], t[1])
+                    bands[side, p, pl.ds(8 * q, 8), 128:256] = jnp.where(lane8 < 96, t[1], t[2])
+            for j in range(10):
+                left = [canvas[p, 0, pl.ds(32 * j + 8 * q, 8), :] for q in range(4)]
+                right = [canvas[p, 2, pl.ds(32 * j + 8 * q, 8), :] for q in range(4)]
+                strips[0, p, pl.ds(8 * j, 8), :] = pack(left, 0)
+                strips[1, p, pl.ds(8 * j, 8), :] = pack(right, 96)
+
+    def send_edges(planes, base):
+        at = pl.ds(planes[0], len(planes))
+        moves = (
+            (bands.at[0, at], from_ns.at[1, at]),
+            (bands.at[1, at], from_ns.at[0, at]),
+            (strips.at[0, at, 8:72, :], from_we.at[1, at]),
+            (strips.at[1, at, 8:72, :], from_we.at[0, at]),
+            (strips.at[0, at, 0:8, :], from_corner.at[3, at]),
+            (strips.at[1, at, 0:8, :], from_corner.at[2, at]),
+            (strips.at[0, at, 72:80, :], from_corner.at[1, at]),
+            (strips.at[1, at, 72:80, :], from_corner.at[0, at]),
+        )
+        return [
+            send(moves[i][0], moves[i][1], send_edge.at[base + i], recv_edge.at[base + i], around[i])
+            for i in (4, 5, 6, 7, 0, 1, 2, 3)
+        ]
+
+    gather_canvas((2,))
+    pack_edges((2,))
+    loads[3].wait()
 
     def put(p, row, centre, west, east):
         t0, t1 = pltpu.roll(centre[0], 32, 1), pltpu.roll(centre[1], 32, 1)
@@ -331,6 +367,8 @@
                 west = strip(halo_we, (0, p, pl.ds(8 * j, 8)), q, 0, has_w)
                 east = strip(halo_we, (1, p, pl.ds(8 * j, 8)), q, 32, has_e)
                 put(p, MARGIN + at, (block[:, :128], block[:, 128:]), west, east)
+
+    edges = send_edges((2,), 0)
 
     def halve(f, stage, side, rows_at, value):
         h, l = split(value)
@@ -424,14 +462,6 @@
             src_ref=dst, dst_ref=dst, send_sem=recvs, recv_sem=recvs, device_id=pair, device_id_type=MESH
         ).wait_recv()
 
-    for x_, y_ in behind_plane:
-        arrive(early1_got.at[4 * x_ + y_], recv_e1.at[4 * x_ + y_])
-    total = early1_got[0]
-    for i in range(1, 16):
-        total = total + early1_got[i]
-    early2[z] = total
-    e2 = [send(early2.at[z], early2.at[z], send_e2.at[i], recv_e2.at[z], column[i]) for i in range(7)]
-
     for f in range(FRAMES):
         for parity in range(2):
             for row in range(0, HALF, STEP):
@@ -468,12 +498,6 @@
     c0 = send(acc.at[:, other, :], got0, send_pair.at[1], recv_pair.at[1], pair)
 
     gather_canvas((0, 1))
-    for p in range(3):
-        for side, base in enumerate((0, MARGIN + W)):
-            for q in range(4):
-                t = [pltpu.roll(canvas[p, i, pl.ds(base + 8 * q, 8), :], 96, 1) for i in range(3)]
-                bands[side, p, pl.ds(8 * q, 8), 0:128] = jnp.where(lane8 < 96, t[0], t[1])
-                bands[side, p, pl.ds(8 * q, 8), 128:256] = jnp.where(lane8 < 96, t[1], t[2])
 
     c0.wait_recv()
     for p in range(2):
@@ -483,12 +507,14 @@
         src = part0.at[:, pl.ds(pl.multiple_of(8 * (4 * x_ + y_), 8), 8), :]
         c1.append(send(src, got1.at[i], send_m1.at[i], recv_m1.at[i], plane[i]))
 
-    for p in range(3):
-        for j in range(10):
-            left = [canvas[p, 0, pl.ds(32 * j + 8 * q, 8), :] for q in range(4)]
-            right = [canvas[p, 2, pl.ds(32 * j + 8 * q, 8), :] for q in range(4)]
-            strips[0, p, pl.ds(8 * j, 8), :] = pack(left, 0)
-            strips[1, p, pl.ds(8 * j, 8), :] = pack(right, 96)
+    pack_edges((0, 1))
+    for x_, y_ in behind_plane:
+        arrive(early1_got.at[4 * x_ + y_], recv_e1.at[4 * x_ + y_])
+    total = early1_got[0]
+    for i in range(1, 16):
+        total = total + early1_got[i]
+    early2[z] = total
+    e2 = [send(early2.at[z], early2.at[z], send_e2.at[i], recv_e2.at[z], column[i]) for i in range(7)]
 
     own = pl.ds(pl.multiple_of(8 * k, 8), 8)
     for copy in c1:
@@ -499,19 +525,7 @@
     all2[z] = total
     c2 = [send(all2.at[z], all2.at[z], send_m2.at[i], recv_m2.at[z], column[i]) for i in range(7)]
 
-    moves = (
-        (bands.at[0], from_ns.at[1]),
-        (bands.at[1], from_ns.at[0]),
-        (strips.at[0, :, 8:72, :], from_we.at[1]),
-        (strips.at[1, :, 8:72, :], from_we.at[0]),
-        (strips.at[0, :, 0:8, :], from_corner.at[3]),
-        (strips.at[1, :, 0:8, :], from_corner.at[2]),
-        (strips.at[0, :, 72:80, :], from_corner.at[1]),
-        (strips.at[1, :, 72:80, :], from_corner.at[0]),
-    )
-    edges = [
-        send(moves[i][0], moves[i][1], send_edge.at[i], recv_edge.at[i], around[i]) for i in (4, 5, 6, 7, 0, 1, 2, 3)
-    ]
+    edges += send_edges((0, 1), 8)
 
     for d in range(1, 8):
         arrive(early2.at[lax.rem(z + d, 8)], recv_e2.at[lax.rem(z + d, 8)])
@@ -587,21 +601,32 @@
         copy.wait_send()
 
 
+def write_kernel(obj, probe, out_obj, out_probe, sems):
+    copies = [
+        pltpu.make_async_copy(obj, out_obj, sems.at[0]),
+        pltpu.make_async_copy(probe, out_probe, sems.at[1]),
+    ]
+    for copy in copies:
+        copy.start()
+    for copy in copies:
+        copy.wait()
+
+
 def vmem(*shape, dtype=F32):
     return pltpu.VMEM(shape, dtype)
 
 
 def per_device(rows, cols, object_field, probe, amplitudes, positions):
     in_vmem = pl.BlockSpec(memory_space=pltpu.VMEM)
-    in_smem = pl.BlockSpec(memory_space=pltpu.SMEM)
-    in_hbm = pl.BlockSpec(memory_space=pl.ANY)
+    in_hbm = pl.BlockSpec(memory_space=pltpu.HBM)
     dma = pltpu.SemaphoreType.DMA
-    return pl.pallas_call(
+    results = pl.pallas_call(
         functools.partial(kernel, rows, cols),
         out_shape=(jax.ShapeDtypeStruct((2, W, W), F32),) * 2,
-        in_specs=[in_smem] + [in_hbm] * 5,
+        in_specs=[in_hbm] * 6,
         out_specs=(in_vmem,) * 2,
         scratch_shapes=[
+            pltpu.SMEM((1, 1, 2, FRAMES), jnp.int32),
             vmem(2, W, W),
             vmem(2, W, W),
             vmem(FRAMES, 2, W, 128),
@@ -635,12 +660,12 @@
             vmem(15, 2, 8, W),
             vmem(8, 2, 8, W),
             vmem(2, W, W),
-            dma((4,)),
+            dma((5,)),
             dma((2 * FRAMES,)),
             dma((8,)),
             dma((8,)),
-            dma((8,)),
-            dma((8,)),
+            dma((16,)),
+            dma((16,)),
             dma((2,)),
             dma((2,)),
             dma((15,)),
@@ -657,17 +682,31 @@
             dma((16,)),
         ],
         compiler_params=pltpu.CompilerParams(
-            collective_id=0, has_side_effects=True, vmem_limit_bytes=56 * 2**20
+            collective_id=0, has_side_effects=True, vmem_limit_bytes=48 * 2**20
         ),
         name="ptycho",
     )(
-        jnp.swapaxes(positions, 2, 3),
-        object_field,
-        probe,
-        amplitudes,
-        jnp.asarray(dft_tables()),
-        jnp.asarray(sort_table()),
+        *(
+            pltpu.with_memory_space_constraint(a, pltpu.HBM)
+            for a in (
+                jnp.swapaxes(positions, 2, 3),
+                object_field,
+                probe,
+                amplitudes,
+                jnp.asarray(dft_tables()),
+                jnp.asarray(sort_table()),
+            )
+        ),
     )
+    return pl.pallas_call(
+        write_kernel,
+        out_shape=(jax.ShapeDtypeStruct((2, W, W), F32),) * 2,
+        in_specs=[in_vmem] * 2,
+        out_specs=(in_hbm,) * 2,
+        scratch_shapes=[dma((2,))],
+        compiler_params=pltpu.CompilerParams(vmem_limit_bytes=2**20),
+        name="write",
+    )(*results)
 
 
 def solution(mesh):

time: 54.7 us -> 46.3 us (0.85)
  Pallas kernels: 51.2 us -> 45.6 us
  local copies, waits for them, and re-layouts: 2.72 us -> 0 us
    pallas_call x1, Pallas kernels: 51.2 us -> 44.6 us  [per_device(): pl.pallas_call(functools.partial(kernel, rows, cols), out_shape=(jax.Shap...]
    unnamed x4 -> x0, local copies, waits for them, and re-layouts: 2.72 us -> none
    pallas_call x0 -> x1, Pallas kernels: none -> 0.99 us  [per_device(): pl.pallas_call(write_kernel, out_shape=(jax.ShapeDtypeStruct((2, W, W), F...]
where the time goes in v3:
time: 46.3 us; the launch traced here: 46.2 us
  Pallas kernels  45.6 us (98%)
  between operations  0.64 us (1%)
    pallas_call x1, Pallas kernels, per_device(): pl.pallas_call(functools.partial(kernel, rows, cols), out_shape=(jax.Shap...  44.6 us
    pallas_call x1, Pallas kernels, per_device(): pl.pallas_call(write_kernel, out_shape=(jax.ShapeDtypeStruct((2, W, W), F...  0.99 us

profile of v3, /device:TPU:1, one launch (start us, length us, event | category | flops | bytes accessed | tf_op | source)
XLA Modules:
  0.0 46.2 jit_solution(1281602544926250395)
XLA Ops:
  0.6 44.6 %ptycho.1 = (f32[2,256,256]{2,1,0:T(8,128)S(1)}, f32[2,256,256]{2,1,0:T(8,128)S(1)}) custom-call(s32[1,1,2,4]{3,2,1,0:T(2,128)} %bitcast.1, f32[2,256,256]{2,1,0:T(8,128)} %obj_hbm.1, f32[2,256,256]{2,1,0:T(8,128)} %probe_hbm.1, f32[1,1,4,256,256]{4,3,2,1,0:T(8,128)} %amps_hbm.1, bf16[4,2,256,256]{3,2,1,0:T(8,128)(2,1)} %constant.4.clone.table_hbm, ...), custom_call_target="tpu_custom_call" | custom-call | tf_op jit(solution)/shard_map/ptycho/pallas_call | solution.py:623
  45.3 1.0 %write.1 = (f32[2,256,256]{2,1,0:T(8,128)}, f32[2,256,256]{2,1,0:T(8,128)}) custom-call(f32[2,256,256]{2,1,0:T(8,128)S(1)} %get-tuple-element.4.obj, f32[2,256,256]{2,1,0:T(8,128)S(1)} %get-tuple-element.5.probe), custom_call_target="tpu_custom_call" | custom-call | tf_op jit(solution)/shard_map/write/pallas_call | solution.py:701

commit v4 on v3

--- a/solution.py
+++ b/solution.py
@@ -114,6 +114,7 @@
     ext,
     spread,
     win,
+    wave,
     sorted_amp,
     half,
     mid,
@@ -168,7 +169,7 @@
         for t in range(2):
             amp_loads.append(
                 pltpu.make_async_copy(
-                    amps_hbm.at[0, 0, f, :, 128 * t : 128 * t + 128], amps.at[f, t], amp_sem.at[2 * f + t]
+                    amps_hbm.at[0, 0, f, :, 128 * t : 128 * t + 128], amps.at[f, t], amp_sem
                 )
             )
 
@@ -183,12 +184,13 @@
     around = neighbours(r, c, rows, cols)
     pair = place(1 - core, x, y, z)
     steps_xy = [(2, 2), (1, 2), (3, 2), (2, 1), (2, 3), (1, 1), (1, 3), (3, 1), (3, 3), (2, 0), (0, 2), (1, 0), (3, 0), (0, 1), (0, 3)]
+    far = [min(dx, 4 - dx) + min(dy, 4 - dy) - 1 for dx, dy in steps_xy]
     on_plane = [(lax.rem(x + dx, 4), lax.rem(y + dy, 4)) for dx, dy in steps_xy]
     behind_plane = [(lax.rem(x + 4 - dx, 4), lax.rem(y + 4 - dy, 4)) for dx, dy in steps_xy]
     plane = [place(core, x_, y_, z) for x_, y_ in on_plane]
     steps_z = [4, 3, 5, 2, 6, 1, 7]
     column = [place(core, x, y, lax.rem(z + d, 8)) for d in steps_z]
-    everyone = around + [pair] + plane + column
+    everyone = column[:1] + plane[:1] + around[4:] + column[1:3] + plane[1:5] + around[:4] + plane[5:] + column[3:] + [pair]
     barrier = pltpu.get_barrier_semaphore()
     for partner in everyone:
         pl.semaphore_signal(barrier, inc=1, device_id=partner, device_id_type=MESH)
@@ -198,6 +200,19 @@
     for load in amp_loads:
         load.start()
     loads[3].start()
+
+    def arrive(dst, recvs):
+        pltpu.make_async_remote_copy(
+            src_ref=dst, dst_ref=dst, send_sem=recvs, recv_sem=recvs, device_id=pair, device_id_type=MESH
+        ).wait_recv()
+
+    def sent(src, sends):
+        pltpu.make_async_remote_copy(
+            src_ref=src, dst_ref=src, send_sem=sends, recv_sem=sends, device_id=pair, device_id_type=MESH
+        ).wait_send()
+
+    def room(count):
+        return mid.at[0, 0, 0 : count // W, :]
 
     loads[0].wait()
     for p in range(2):
@@ -217,9 +232,8 @@
         (halo_strips.at[0, :, 56:64, :], halo_corner.at[1]),
         (halo_strips.at[1, :, 56:64, :], halo_corner.at[0]),
     )
-    halo = [
-        send(moves[i][0], moves[i][1], send_halo.at[i], recv_halo.at[i], around[i]) for i in (4, 5, 6, 7, 0, 1, 2, 3)
-    ]
+    for i in (4, 5, 6, 7, 0, 1, 2, 3):
+        send(moves[i][0], moves[i][1], send_halo, recv_halo.at[int(i in (2, 3))], around[i])
 
     lane = lanes(STEP)
     zero = jnp.zeros((STEP, 128), F32)
@@ -236,10 +250,9 @@
     loads[1].wait()
     loads[4].wait()
     loads[2].wait()
+    pltpu.make_async_copy(amps, amps, amp_sem).wait()
     sums = jnp.zeros((8, 128), F32)
     for f in range(FRAMES):
-        amp_loads[2 * f].wait()
-        amp_loads[2 * f + 1].wait()
         parts = []
         for parity in (0, 1):
             a = jnp.concatenate([amps[f, t, pl.ds(parity, HALF, stride=2), :] for t in range(2)], axis=1)
@@ -323,7 +336,7 @@
                 strips[0, p, pl.ds(8 * j, 8), :] = pack(left, 0)
                 strips[1, p, pl.ds(8 * j, 8), :] = pack(right, 96)
 
-    def send_edges(planes, base):
+    def send_edges(planes):
         at = pl.ds(planes[0], len(planes))
         moves = (
             (bands.at[0, at], from_ns.at[1, at]),
@@ -335,10 +348,8 @@
             (strips.at[0, at, 72:80, :], from_corner.at[1, at]),
             (strips.at[1, at, 72:80, :], from_corner.at[0, at]),
         )
-        return [
-            send(moves[i][0], moves[i][1], send_edge.at[base + i], recv_edge.at[base + i], around[i])
-            for i in (4, 5, 6, 7, 0, 1, 2, 3)
-        ]
+        for i in (4, 5, 6, 7, 0, 1, 2, 3):
+            send(moves[i][0], moves[i][1], send_edge, recv_edge, around[i])
 
     gather_canvas((2,))
     pack_edges((2,))
@@ -350,8 +361,45 @@
         ext[p, 1, pl.ds(row, 8), :] = jnp.where(first, t0, t1)
         ext[p, 2, pl.ds(row, 8), :] = jnp.where(first, t1, jnp.where(second, east, zero8))
 
-    for copy in halo:
-        copy.wait_recv()
+    arrive(room(2 * 2 * 64 * 128), recv_halo.at[1])
+    for p in range(2):
+        for j in range(8):
+            for q in range(4):
+                at = 32 * j + 8 * q
+                block = obj[p, pl.ds(at, 8), :]
+                west = strip(halo_we, (0, p, pl.ds(8 * j, 8)), q, 0, has_w)
+                east = strip(halo_we, (1, p, pl.ds(8 * j, 8)), q, 32, has_e)
+                put(p, MARGIN + at, (block[:, :128], block[:, 128:]), west, east)
+    def halve(f, stage, side, rows_at, value):
+        h, l = split(value)
+        half[stage, side, 0, pl.ds(W * f + rows_at.start, rows_at.size), :] = h
+        half[stage, side, 1, pl.ds(W * f + rows_at.start, rows_at.size), :] = l
+
+    def first_step(some_rows):
+        for row in some_rows:
+            sums = [jnp.zeros((STEP, W), F32)] * 2
+            for f in range(FRAMES):
+                waves = []
+                for i, base in enumerate((row, HALF + row)):
+                    here = pl.ds(base, STEP)
+                    wr, wi = gather(f, 0, base), gather(f, 1, base)
+                    pr, pi = probe[0, here, :], probe[1, here, :]
+                    win[f, 0, here, :] = wr
+                    win[f, 1, here, :] = wi
+                    sums[i] = sums[i] + (wr * wr + wi * wi)
+                    waves.append((pr * wr - pi * wi, pr * wi + pi * wr))
+                    wave[f, 0, here, :], wave[f, 1, here, :] = waves[-1]
+                for part in range(2):
+                    top, low = waves[0][part], waves[1][part]
+                    where = pl.ds(HALF * part + row, STEP)
+                    halve(f, 0, 0, where, top + low)
+                    halve(f, 0, 1, where, top - low)
+            for i, base in enumerate((row, HALF + row)):
+                power2[pl.ds(base, STEP), :] = sums[i][:, :128]
+                power2[pl.ds(W + base, STEP), :] = sums[i][:, 128:]
+
+    first_step(range(MARGIN, HALF - MARGIN, STEP))
+    arrive(room(2 * 2 * 32 * W + 4 * 2 * 8 * 128), recv_halo.at[0])
     for p in range(2):
         for k in range(4):
             for side, (keep_v, base) in enumerate(((has_n, 0), (has_s, MARGIN + W))):
@@ -360,41 +408,9 @@
                 west = strip(halo_corner, (2 * side, p, slice(0, 8)), k, 0, has_w & keep_v)
                 east = strip(halo_corner, (2 * side + 1, p, slice(0, 8)), k, 32, has_e & keep_v)
                 put(p, base + 8 * k, (block[:, :128], block[:, 128:]), west, east)
-        for j in range(8):
-            for q in range(4):
-                at = 32 * j + 8 * q
-                block = obj[p, pl.ds(at, 8), :]
-                west = strip(halo_we, (0, p, pl.ds(8 * j, 8)), q, 0, has_w)
-                east = strip(halo_we, (1, p, pl.ds(8 * j, 8)), q, 32, has_e)
-                put(p, MARGIN + at, (block[:, :128], block[:, 128:]), west, east)
-
-    edges = send_edges((2,), 0)
-
-    def halve(f, stage, side, rows_at, value):
-        h, l = split(value)
-        half[f, stage, side, 0, rows_at, :] = h
-        half[f, stage, side, 1, rows_at, :] = l
-
-    for row in range(0, HALF, STEP):
-        sums = [jnp.zeros((STEP, W), F32)] * 2
-        for f in range(FRAMES):
-            waves = []
-            for i, base in enumerate((row, HALF + row)):
-                here = pl.ds(base, STEP)
-                wr, wi = gather(f, 0, base), gather(f, 1, base)
-                pr, pi = probe[0, here, :], probe[1, here, :]
-                win[f, 0, here, :] = wr
-                win[f, 1, here, :] = wi
-                sums[i] = sums[i] + (wr * wr + wi * wi)
-                waves.append((pr * wr - pi * wi, pr * wi + pi * wr))
-            for part in range(2):
-                top, low = waves[0][part], waves[1][part]
-                where = pl.ds(HALF * part + row, STEP)
-                halve(f, 0, 0, where, top + low)
-                halve(f, 0, 1, where, top - low)
-        for i, base in enumerate((row, HALF + row)):
-            power2[pl.ds(base, STEP), :] = sums[i][:, :128]
-            power2[pl.ds(W + base, STEP), :] = sums[i][:, 128:]
+
+    send_edges((2,))
+    first_step([*range(0, MARGIN, STEP), *range(HALF - MARGIN, HALF, STEP)])
 
     mine8 = pl.multiple_of(core * HALF, HALF)
     other8 = pl.multiple_of((1 - core) * HALF, HALF)
@@ -404,26 +420,26 @@
 
     def left_dots(stage, flip):
         for f in range(FRAMES):
+            here = pl.ds(W * f, W)
             for side in range(2):
-                mid[f, stage, side] = triple(
+                mid[stage, side, here, :] = triple(
                     (table[flip + side, 0], table[flip + side, 1]),
-                    (half[f, stage, side, 0], half[f, stage, side, 1]),
+                    (half[stage, side, 0, here, :], half[stage, side, 1, here, :]),
                 )
 
     def right_dots(stage, flip):
-        for f in range(FRAMES):
-            for side in range(2):
-                mid[f, stage, side] = triple(
-                    (half[f, stage, side, 0], half[f, stage, side, 1]),
-                    (table[flip + side, 0], table[flip + side, 1]),
-                )
+        for side in range(2):
+            mid[stage, side] = triple(
+                (half[stage, side, 0], half[stage, side, 1]),
+                (table[flip + side, 0], table[flip + side, 1]),
+            )
 
     left_dots(0, 0)
     for f in range(FRAMES):
         for parity in range(2):
             for row in range(0, HALF, STEP):
-                zr = mid[f, 0, parity, pl.ds(row, STEP), :]
-                zi = mid[f, 0, parity, pl.ds(HALF + row, STEP), :]
+                zr = mid[0, parity, pl.ds(W * f + row, STEP), :]
+                zi = mid[0, parity, pl.ds(W * f + HALF + row, STEP), :]
                 here = pl.ds(HALF * parity + row, STEP)
                 plus = jnp.concatenate([zr[:, :128] + zr[:, 128:], zi[:, :128] + zi[:, 128:]], axis=1)
                 less = jnp.concatenate([zr[:, :128] - zr[:, 128:], zi[:, :128] - zi[:, 128:]], axis=1)
@@ -442,7 +458,7 @@
     early1_got[k] = early1[k]
     e1 = []
     for i, (x_, y_) in enumerate(on_plane):
-        e1.append(send(early1.at[4 * x_ + y_], early1_got.at[k], send_e1.at[i], recv_e1.at[k], plane[i]))
+        e1.append(send(early1.at[4 * x_ + y_], early1_got.at[k], send_e1.at[0], recv_e1.at[0], plane[i]))
 
     right_dots(1, 2)
     for f in range(FRAMES):
@@ -450,23 +466,17 @@
             for row in range(0, W, STEP):
                 here = pl.ds(row, STEP)
                 amp = sorted_amp[f, here, 128 * side : 128 * side + 128]
-                v = mid[f, 1, side, here, :]
+                v = mid[1, side, pl.ds(W * f + row, STEP), :]
                 zr, zi = v[:, :128], v[:, 128:]
                 factor = amp * lax.rsqrt(zr * zr + zi * zi + smoothing)
                 halve(f, 2, side, here, jnp.concatenate([zr * factor, zi * factor], axis=1))
 
     right_dots(2, 0)
 
-    def arrive(dst, recvs):
-        pltpu.make_async_remote_copy(
-            src_ref=dst, dst_ref=dst, send_sem=recvs, recv_sem=recvs, device_id=pair, device_id_type=MESH
-        ).wait_recv()
-
     for f in range(FRAMES):
         for parity in range(2):
             for row in range(0, HALF, STEP):
-                here = pl.ds(HALF * parity + row, STEP)
-                even, odd = mid[f, 2, 0, here, :], mid[f, 2, 1, here, :]
+                even, odd = (mid[2, i, pl.ds(W * f + HALF * parity + row, STEP), :] for i in range(2))
                 plus, less = even + odd, even - odd
                 for part in range(2):
                     cut = slice(128 * part, 128 * part + 128)
@@ -477,8 +487,8 @@
     for row in range(0, HALF, STEP):
         parts = []
         for f in range(FRAMES):
-            er, orr = mid[f, 3, 0, pl.ds(row, STEP), :], mid[f, 3, 1, pl.ds(row, STEP), :]
-            ei, oi = mid[f, 3, 0, pl.ds(HALF + row, STEP), :], mid[f, 3, 1, pl.ds(HALF + row, STEP), :]
+            er, orr = (mid[3, i, pl.ds(W * f + row, STEP), :] for i in range(2))
+            ei, oi = (mid[3, i, pl.ds(W * f + HALF + row, STEP), :] for i in range(2))
             parts.append(((er + orr, ei + oi), (er - orr, ei - oi)))
         for side, base in enumerate((row, HALF + row)):
             here = pl.ds(base, STEP)
@@ -486,8 +496,8 @@
             sums = [jnp.zeros((STEP, W), F32)] * 2
             for f in range(FRAMES):
                 wr, wi = win[f, 0, here, :], win[f, 1, here, :]
-                dr = parts[f][side][0] - (pr * wr - pi * wi)
-                di = parts[f][side][1] - (pr * wi + pi * wr)
+                dr = parts[f][side][0] - wave[f, 0, here, :]
+                di = parts[f][side][1] - wave[f, 1, here, :]
                 scatter(f, 0, base, pr * dr + pi * di)
                 scatter(f, 1, base, pr * di - pi * dr)
                 sums = [sums[0] + (wr * dr + wi * di), sums[1] + (wr * di - wi * dr)]
@@ -495,40 +505,44 @@
 
     mine = pl.ds(mine8, HALF)
     other = pl.ds(other8, HALF)
-    c0 = send(acc.at[:, other, :], got0, send_pair.at[1], recv_pair.at[1], pair)
+    c0 = [
+        send(acc.at[p, other, :], got0.at[p], send_pair.at[1 + p], recv_pair.at[1 + p], pair) for p in range(2)
+    ]
 
     gather_canvas((0, 1))
 
-    c0.wait_recv()
-    for p in range(2):
+    c1 = []
+    for p in range(2):
+        c0[p].wait_recv()
         part0[p] = acc[p, mine, :] + got0[p]
-    c1 = []
-    for i, (x_, y_) in enumerate(on_plane):
-        src = part0.at[:, pl.ds(pl.multiple_of(8 * (4 * x_ + y_), 8), 8), :]
-        c1.append(send(src, got1.at[i], send_m1.at[i], recv_m1.at[i], plane[i]))
+        for i, (x_, y_) in enumerate(on_plane):
+            src = part0.at[p, pl.ds(pl.multiple_of(8 * (4 * x_ + y_), 8), 8), :]
+            c1.append(send(src, got1.at[p, i], send_m1.at[p], recv_m1.at[p], plane[i]))
 
     pack_edges((0, 1))
-    for x_, y_ in behind_plane:
-        arrive(early1_got.at[4 * x_ + y_], recv_e1.at[4 * x_ + y_])
+    arrive(early1_got.at[0:15], recv_e1.at[0])
     total = early1_got[0]
     for i in range(1, 16):
         total = total + early1_got[i]
     early2[z] = total
-    e2 = [send(early2.at[z], early2.at[z], send_e2.at[i], recv_e2.at[z], column[i]) for i in range(7)]
+    e2 = [send(early2.at[z], early2.at[z], send_e2.at[0], recv_e2.at[0], column[i]) for i in range(7)]
 
     own = pl.ds(pl.multiple_of(8 * k, 8), 8)
-    for copy in c1:
-        copy.wait_recv()
-    total = part0[:, own, :]
-    for i in range(15):
-        total = total + got1[i]
-    all2[z] = total
-    c2 = [send(all2.at[z], all2.at[z], send_m2.at[i], recv_m2.at[z], column[i]) for i in range(7)]
-
-    edges += send_edges((0, 1), 8)
-
-    for d in range(1, 8):
-        arrive(early2.at[lax.rem(z + d, 8)], recv_e2.at[lax.rem(z + d, 8)])
+    c2 = []
+    for p in range(2):
+        arrive(got1.at[p], recv_m1.at[p])
+        total = part0[p, own, :]
+        for i in range(15):
+            total = total + got1[p, i]
+        all2[p, z] = total
+        for i in range(7):
+            c2.append(
+                send(all2.at[p, z], all2.at[p, z], send_m2.at[p], recv_m2.at[p], column[i])
+            )
+
+    send_edges((0, 1))
+
+    arrive(early2.at[0:7], recv_e2.at[0])
     total = early2[0]
     for i in range(1, 8):
         total = total + early2[i]
@@ -536,21 +550,26 @@
     target = jnp.sum(total[16:24]) * (1.0 / (FRAMES * rows * cols))
 
     block = pl.ds(pl.multiple_of(HALF * core + 8 * k, 8), 8)
-    for d in range(1, 8):
-        arrive(all2.at[lax.rem(z + d, 8)], recv_m2.at[lax.rem(z + d, 8)])
-    total = all2[0]
-    for i in range(1, 8):
-        total = total + all2[i]
-    for p in range(2):
-        gathered[p, block, :] = probe[p, block, :] + total[p] * weight
-    g1 = [
-        send(gathered.at[:, block, :], gathered.at[:, block, :], send_ag.at[i], recv_ag.at[i], plane[i])
-        for i in range(15)
-    ]
-    fw = [send(gathered.at[:, block, :], gathered.at[:, block, :], send_fw.at[15], recv_fw.at[15], pair)]
-
-    for copy in edges:
-        copy.wait_recv()
+    for p in range(2):
+        arrive(all2.at[p, 0:7], recv_m2.at[p])
+        total = all2[p, 0]
+        for i in range(1, 8):
+            total = total + all2[p, i]
+        gathered[p, block, :] = probe[p, block, :] + total * weight
+        here = gathered.at[p, block, :]
+        for i in range(15):
+            send(here, here, send_ag.at[p], recv_ag.at[4 * p + far[i]], plane[i])
+        send(here, here, send_fw.at[p], recv_fw.at[p], pair)
+
+    for p in range(2):
+        for distance in range(4):
+            batch = [i for i in range(15) if far[i] == distance]
+            arrive(gathered.at[p, 0 : 8 * len(batch)], recv_ag.at[4 * p + distance])
+            for i in batch:
+                x_, y_ = behind_plane[i]
+                here = gathered.at[p, pl.ds(pl.multiple_of(HALF * core + 8 * (4 * x_ + y_), 8), 8), :]
+                send(here, here, send_fw.at[p], recv_fw.at[p], pair)
+    arrive(room(3 * (2 * 32 * W + 2 * 64 * 128 + 4 * 8 * 128)), recv_edge)
     for j in range(8):
         for q in range(4):
             at = 32 * j + 8 * q
@@ -580,15 +599,18 @@
                     here = (p, pl.ds(at, 8), slice(128 * s, 128 * s + 128))
                     out_obj[here] = obj[here] + totals[p][s] * scale
 
-    for i in reversed(range(15)):
-        x_, y_ = behind_plane[i]
-        at = pl.ds(pl.multiple_of(HALF * core + 8 * (4 * x_ + y_), 8), 8)
-        arrive(gathered.at[:, at, :], recv_ag.at[i])
-        fw.append(send(gathered.at[:, at, :], gathered.at[:, at, :], send_fw.at[i], recv_fw.at[i], pair))
-    for i in range(16):
-        x_, y_ = behind_plane[i] if i < 15 else (x, y)
-        at = pl.ds(pl.multiple_of(HALF * (1 - core) + 8 * (4 * x_ + y_), 8), 8)
-        arrive(gathered.at[:, at, :], recv_fw.at[i])
+    for copy in [e0] + c0:
+        copy.wait_send()
+    sent(room(2 * (2 * 32 * W + 2 * 64 * 128 + 4 * 8 * 128)), send_halo)
+    sent(room(3 * (2 * 32 * W + 2 * 64 * 128 + 4 * 8 * 128)), send_edge)
+    sent(early1.at[0:15], send_e1.at[0])
+    sent(early2.at[0:7], send_e2.at[0])
+    for p in range(2):
+        sent(got1.at[p], send_m1.at[p])
+        sent(all2.at[p, 0:7], send_m2.at[p])
+
+    for p in range(2):
+        arrive(gathered.at[p, other, :], recv_fw.at[p])
     power = jnp.zeros((8, W), F32)
     for p in range(2):
         g = gathered[p]
@@ -597,8 +619,9 @@
     for p in range(2):
         out_probe[p] = gathered[p] * jnp.concatenate([scale] * 32, axis=0)
 
-    for copy in halo + [e0, c0] + e1 + e2 + c1 + c2 + edges + g1 + fw:
-        copy.wait_send()
+    for p in range(2):
+        sent(gathered.at[p, 0:120], send_ag.at[p])
+        sent(gathered.at[p, mine, :], send_fw.at[p])
 
 
 def write_kernel(obj, probe, out_obj, out_probe, sems):
@@ -639,9 +662,10 @@
             vmem(2, 3, SIDE, 128),
             vmem(FRAMES, 3, 3, LEAD + W + LEAD, 128),
             vmem(FRAMES, 2, W, W),
+            vmem(FRAMES, 2, W, W),
             vmem(FRAMES, W, W),
-            vmem(FRAMES, 4, 2, 2, W, W, dtype=BF16),
-            vmem(FRAMES, 4, 2, W, W),
+            vmem(4, 2, 2, FRAMES * W, W, dtype=BF16),
+            vmem(4, 2, FRAMES * W, W),
             vmem(2, W, W),
             vmem(2 * W, 128),
             vmem(3, 3, SIDE, 128),
@@ -657,29 +681,29 @@
             vmem(8, 24, 128),
             vmem(2, HALF, W),
             vmem(2, HALF, W),
-            vmem(15, 2, 8, W),
-            vmem(8, 2, 8, W),
+            vmem(2, 15, 8, W),
+            vmem(2, 8, 8, W),
             vmem(2, W, W),
             dma((5,)),
-            dma((2 * FRAMES,)),
-            dma((8,)),
-            dma((8,)),
-            dma((16,)),
-            dma((16,)),
+            dma,
+            dma,
+            dma((2,)),
+            dma,
+            dma,
+            dma((3,)),
+            dma((3,)),
+            dma((1,)),
+            dma((1,)),
+            dma((1,)),
+            dma((1,)),
             dma((2,)),
             dma((2,)),
-            dma((15,)),
-            dma((16,)),
-            dma((7,)),
+            dma((2,)),
+            dma((2,)),
+            dma((2,)),
             dma((8,)),
-            dma((15,)),
-            dma((15,)),
-            dma((7,)),
-            dma((8,)),
-            dma((15,)),
-            dma((15,)),
-            dma((16,)),
-            dma((16,)),
+            dma((2,)),
+            dma((2,)),
         ],
         compiler_params=pltpu.CompilerParams(
             collective_id=0, has_side_effects=True, vmem_limit_bytes=48 * 2**20

time: 46.3 us -> 42.7 us (0.922)
  Pallas kernels: 45.6 us -> 41.9 us
    pallas_call x1, Pallas kernels: 44.6 us -> 41 us  [per_device(): pl.pallas_call(functools.partial(kernel, rows, cols), out_shape=(jax.Shap...]
where the time goes in v4:
time: 42.7 us; the launch traced here: 42.6 us
  Pallas kernels  41.9 us (98%)
  between operations  0.64 us (1%)
    pallas_call x1, Pallas kernels, per_device(): pl.pallas_call(functools.partial(kernel, rows, cols), out_shape=(jax.Shap...  41 us
    pallas_call x1, Pallas kernels, per_device(): pl.pallas_call(write_kernel, out_shape=(jax.ShapeDtypeStruct((2, W, W), F...  0.99 us

profile of v4, /device:TPU:1, one launch (start us, length us, event | category | flops | bytes accessed | tf_op | source)
XLA Modules:
  0.0 42.6 jit_solution(9683239648648503107)
XLA Ops:
  0.6 41.0 %ptycho.1 = (f32[2,256,256]{2,1,0:T(8,128)S(1)}, f32[2,256,256]{2,1,0:T(8,128)S(1)}) custom-call(s32[1,1,2,4]{3,2,1,0:T(2,128)} %bitcast.1, f32[2,256,256]{2,1,0:T(8,128)} %obj_hbm.1, f32[2,256,256]{2,1,0:T(8,128)} %probe_hbm.1, f32[1,1,4,256,256]{4,3,2,1,0:T(8,128)} %amps_hbm.1, bf16[4,2,256,256]{3,2,1,0:T(8,128)(2,1)} %constant.4.clone.table_hbm, ...), custom_call_target="tpu_custom_call" | custom-call | tf_op jit(solution)/shard_map/ptycho/pallas_call | solution.py:646
  41.6 1.0 %write.1 = (f32[2,256,256]{2,1,0:T(8,128)}, f32[2,256,256]{2,1,0:T(8,128)}) custom-call(f32[2,256,256]{2,1,0:T(8,128)S(1)} %get-tuple-element.4.obj, f32[2,256,256]{2,1,0:T(8,128)S(1)} %get-tuple-element.5.probe), custom_call_target="tpu_custom_call" | custom-call | tf_op jit(solution)/shard_map/write/pallas_call | solution.py:725

commit v5 on v4

--- a/solution.py
+++ b/solution.py
@@ -446,6 +446,17 @@
                 halve(f, 1, 0, here, plus)
                 halve(f, 1, 1, here, less)
 
+    right_dots(1, 2)
+    for f in range(FRAMES):
+        for side in range(2):
+            for row in range(0, W, STEP):
+                here = pl.ds(row, STEP)
+                amp = sorted_amp[f, here, 128 * side : 128 * side + 128]
+                v = mid[1, side, pl.ds(W * f + row, STEP), :]
+                zr, zi = v[:, :128], v[:, 128:]
+                factor = amp * lax.rsqrt(zr * zr + zi * zi + smoothing)
+                halve(f, 2, side, here, jnp.concatenate([zr * factor, zi * factor], axis=1))
+
     k = 4 * x + y
     e0.wait_recv()
     for i in range(16):
@@ -459,17 +470,6 @@
     e1 = []
     for i, (x_, y_) in enumerate(on_plane):
         e1.append(send(early1.at[4 * x_ + y_], early1_got.at[k], send_e1.at[0], recv_e1.at[0], plane[i]))
-
-    right_dots(1, 2)
-    for f in range(FRAMES):
-        for side in range(2):
-            for row in range(0, W, STEP):
-                here = pl.ds(row, STEP)
-                amp = sorted_amp[f, here, 128 * side : 128 * side + 128]
-                v = mid[1, side, pl.ds(W * f + row, STEP), :]
-                zr, zi = v[:, :128], v[:, 128:]
-                factor = amp * lax.rsqrt(zr * zr + zi * zi + smoothing)
-                halve(f, 2, side, here, jnp.concatenate([zr * factor, zi * factor], axis=1))
 
     right_dots(2, 0)
 

time: 42.7 us -> 42.6 us (level)
  no operation moved by 1% of the time
where the time goes in v5:
time: 42.6 us
  Pallas kernels  42 us (99%)
  between operations  0.64 us (2%)
    pallas_call x1, Pallas kernels, per_device(): pl.pallas_call(functools.partial(kernel, rows, cols), out_shape=(jax.Shap...  41 us
    pallas_call x1, Pallas kernels, per_device(): pl.pallas_call(write_kernel, out_shape=(jax.ShapeDtypeStruct((2, W, W), F...  0.99 us

profile of v5, /device:TPU:1, one launch (start us, length us, event | category | flops | bytes accessed | tf_op | source)
XLA Modules:
  0.0 42.6 jit_solution(4791530924935058654)
XLA Ops:
  0.6 41.0 %ptycho.1 = (f32[2,256,256]{2,1,0:T(8,128)S(1)}, f32[2,256,256]{2,1,0:T(8,128)S(1)}) custom-call(s32[1,1,2,4]{3,2,1,0:T(2,128)} %bitcast.1, f32[2,256,256]{2,1,0:T(8,128)} %obj_hbm.1, f32[2,256,256]{2,1,0:T(8,128)} %probe_hbm.1, f32[1,1,4,256,256]{4,3,2,1,0:T(8,128)} %amps_hbm.1, bf16[4,2,256,256]{3,2,1,0:T(8,128)(2,1)} %constant.4.clone.table_hbm, ...), custom_call_target="tpu_custom_call" | custom-call | tf_op jit(solution)/shard_map/ptycho/pallas_call | solution.py:646
  41.6 1.0 %write.1 = (f32[2,256,256]{2,1,0:T(8,128)}, f32[2,256,256]{2,1,0:T(8,128)}) custom-call(f32[2,256,256]{2,1,0:T(8,128)S(1)} %get-tuple-element.4.obj, f32[2,256,256]{2,1,0:T(8,128)S(1)} %get-tuple-element.5.probe), custom_call_target="tpu_custom_call" | custom-call | tf_op jit(solution)/shard_map/write/pallas_call | solution.py:725
